TPU v7x, 128 devices: a whole 4x4x4 slice. The times are simulated.
128 devices in a mesh: seq: 16 (over x_hi, y, core), tp: 8 (over x_lo, z).
Axes of the slice: x: 4 (x_hi: 2, x_lo: 2; x = x_hi * 2 + x_lo), y: 4, z: 4, core: 2. Of those that a mesh axis runs over, the one named last changes fastest.
Arguments:
- tokens: bfloat16 [8192, 1024], P('seq'), may hold values from -6 to 6
- segment_ids: int32 [8192], P('seq'), may hold values from 0 to 63, never falling along the last dimension, each value on 1 to 4608 neighbouring positions
- prefix_cache: bfloat16 [16384, 8, 128], P('seq', 'tp'), may hold values from -320 to 320
- norm1_gain: float32 [1024], replicated, may hold values from 0.5 to 1.5
- w_qkv: bfloat16 [1024, 8, 256], P(None, 'tp'), may hold values from -0.875 to 0.875
- w_out: bfloat16 [8, 128, 1024], P('tp'), may hold values from -0.1875 to 0.1875
- norm2_gain: float32 [1024], replicated, may hold values from 0.5 to 1.5
- expert_in: bfloat16 [32, 1024, 1024], P('seq'), may hold values from -0.1875 to 0.1875
- expert_out: bfloat16 [32, 512, 1024], P('seq'), may hold values from -0.25 to 0.25
- routes: int32 [8192, 8], P(('seq', 'tp')), may hold values from 0 to 31, all different within a row; in each aligned block of 64 rows (0 to 63, 64 to 127, ...) at most 32 rows name the same one
- route_weights: float32 [8192, 8], P(('seq', 'tp')), may hold values from 0.05 to 0.25
Outputs:
- hidden_out: bfloat16 [8192, 1024], P(('seq', 'tp'))
- new_cache: bfloat16 [8192, 8, 128], P('seq', 'tp')
Inputs may be any that keep to these rules, and one draw needn't show every extreme that they name: `segment_ids`: 64 requests lie in order of their numbers, each on 1 to 4608 consecutive new tokens, one on exactly that many. `routes`: each row names 8 different experts; in the rows of one device (aligned blocks of 64 rows) no expert is named by more than 32 rows, a bound that some block reaches.
All inputs are finite; a program needn't handle non-finite values.
Results may differ from a plain program's by a relative error of at most 0.02.
The roundings to bfloat16 on the way count: a program that leaves them out, or rounds other values in their place, can miss the bound.
Values may be sent and summed in bfloat16 or wider, within the bound.
No kernel may reach another device: no remote copies, remote signals or barrier semaphores. Data moves between devices by JAX's collectives and lax.ppermute only.
A program may use at most 128 MiB of HBM per device.

v0:
```python
import math

import jax
import jax.numpy as jnp
from jax import lax
from jax.sharding import PartitionSpec as P

SCORE_SCALE = 0.015625
EPSILON = 1e-06


def normalize(inputs, norm_gain):
    widened = inputs.astype(jnp.float32)
    mean_square = jnp.mean(widened * widened, axis=-1, keepdims=True)
    return widened * lax.rsqrt(mean_square + EPSILON) * norm_gain


def body(
    tokens,
    segment_ids,
    prefix_cache,
    norm1_gain,
    w_qkv,
    w_out,
    norm2_gain,
    expert_in,
    expert_out,
    routes,
    route_weights,
):
    tok_dev = tokens.shape[0]
    kv_loc = w_qkv.shape[1]
    head_dim = prefix_cache.shape[2] // 2
    group_size = w_qkv.shape[2] // head_dim - 2
    width = tokens.shape[1]
    normed = normalize(tokens, norm1_gain).astype(jnp.bfloat16)
    projected = jnp.einsum("td,dkc->tkc", normed, w_qkv, preferred_element_type=jnp.float32)
    queries = (
        projected[:, :, : group_size * head_dim]
        .astype(jnp.bfloat16)
        .reshape(tok_dev, kv_loc, group_size, head_dim)
    )
    new_cache = projected[:, :, group_size * head_dim :].astype(jnp.bfloat16)
    own_start = lax.axis_index("seq") * tok_dev
    query_pos = own_start + jnp.arange(tok_dev, dtype=jnp.int32)
    query_seg = segment_ids.astype(jnp.float32)
    seg_wire = segment_ids.astype(jnp.bfloat16)

    def attend(carried, cache_block, key_pos, key_seg, masked):
        running_max, running_sum, weighted = carried
        key_part = cache_block[:, :, :head_dim]
        value_part = cache_block[:, :, head_dim:]
        scores = (
            jnp.einsum("tkgd,skd->tkgs", queries, key_part, preferred_element_type=jnp.float32)
            * SCORE_SCALE
        )
        if masked:
            usable = (
                (key_seg[None, :] == query_seg[:, None])
                & (key_pos[None, :] <= query_pos[:, None])
                & (key_pos[None, :] >= 0)
            )
            usable = usable[:, None, None, :]
            scores = jnp.where(usable, scores, -1e30)
        new_max = jnp.maximum(running_max, jnp.max(scores, axis=-1))
        weights = jnp.exp(scores - new_max[..., None])
        if masked:
            weights = jnp.where(usable, weights, 0.0)
        rescale = jnp.exp(running_max - new_max)
        running_sum = running_sum * rescale + jnp.sum(weights, axis=-1)
        weighted = weighted * rescale[..., None] + jnp.einsum(
            "tkgs,skd->tkgd",
            weights.astype(jnp.bfloat16),
            value_part,
            preferred_element_type=jnp.float32,
        )
        return (new_max, running_sum, weighted)

    def attend_blocks(carried, cache_rows, key_pos, key_seg, masked):
        length = cache_rows.shape[0]
        block_len = math.gcd(length, 1024)
        blocks = length // block_len
        members = (
            cache_rows.reshape(blocks, block_len, kv_loc, 2 * head_dim),
            key_pos.reshape(blocks, block_len),
            key_seg.reshape(blocks, block_len),
        )

        def scan_step(state, member):
            return (attend(state, member[0], member[1], member[2], masked), None)

        return lax.scan(scan_step, carried, members)[0]

    initial = (
        jnp.full((tok_dev, kv_loc, group_size), -1e30, jnp.float32),
        jnp.zeros((tok_dev, kv_loc, group_size), jnp.float32),
        jnp.zeros((tok_dev, kv_loc, group_size, head_dim), jnp.float32),
    )
    shard_piece = lax.all_gather(prefix_cache, "seq", axis=0, tiled=True)
    length = shard_piece.shape[0]
    prefix_state = attend_blocks(
        initial,
        shard_piece,
        jnp.zeros((length,), jnp.int32),
        jnp.zeros((length,), jnp.float32),
        False,
    )
    cache_piece = lax.all_gather(new_cache, "seq", axis=0, tiled=True)
    seg_piece = lax.all_gather(seg_wire, "seq", axis=0, tiled=True)
    length = cache_piece.shape[0]
    final_state = attend_blocks(
        prefix_state,
        cache_piece,
        jnp.arange(length, dtype=jnp.int32),
        seg_piece.astype(jnp.float32),
        True,
    )
    attended = (final_state[2] / final_state[1][..., None]).astype(jnp.bfloat16)
    flat_attn = attended.reshape(tok_dev, kv_loc * group_size * head_dim)
    row_count = tok_dev // lax.axis_size("tp")
    flat_out = w_out.reshape(kv_loc * group_size * head_dim, width)
    mixed = lax.psum_scatter(
        jnp.dot(flat_attn, flat_out, preferred_element_type=jnp.float32).astype(jnp.bfloat16),
        "tp",
        scatter_dimension=0,
        tiled=True,
    ).astype(jnp.float32)
    own_rows = lax.dynamic_slice_in_dim(
        tokens, lax.axis_index("tp") * row_count, row_count, 0
    ).astype(jnp.float32)
    residual = own_rows + mixed
    expert_input = normalize(residual, norm2_gain).astype(jnp.bfloat16)
    seq_total = lax.axis_size("seq")
    exp_loc = expert_in.shape[0]
    expert_total = seq_total * exp_loc
    capacity = row_count // 2
    top_count = routes.shape[1]
    flat_routes = routes.reshape(-1)
    one_hot = (flat_routes[:, None] == jnp.arange(expert_total, dtype=jnp.int32)[None, :]).astype(
        jnp.int32
    )
    rank_in = jnp.sum(one_hot * (jnp.cumsum(one_hot, axis=0) - 1), axis=1)
    slot_index = flat_routes * capacity + rank_in
    owner_row = jnp.repeat(jnp.arange(row_count, dtype=jnp.int32), top_count)
    slot_table = (
        jnp.full((expert_total * capacity,), row_count, jnp.int32).at[slot_index].set(owner_row)
    )
    padded = jnp.concatenate([expert_input, jnp.zeros((1, width), jnp.bfloat16)], axis=0)
    outgoing = jnp.take(padded, slot_table, axis=0).reshape(seq_total, exp_loc, capacity, width)
    joined = jnp.einsum(
        "secd,edf->secf",
        lax.all_to_all(outgoing, "seq", split_axis=0, concat_axis=0, tiled=True),
        expert_in,
        preferred_element_type=jnp.float32,
    )
    half_width = joined.shape[-1] // 2
    expert_hidden = (jax.nn.silu(joined[..., :half_width]) * joined[..., half_width:]).astype(
        jnp.bfloat16
    )
    answered = jnp.einsum(
        "secf,efd->secd", expert_hidden, expert_out, preferred_element_type=jnp.float32
    ).astype(jnp.bfloat16)
    returned = lax.all_to_all(answered, "seq", split_axis=0, concat_axis=0, tiled=True)
    picked = jnp.take(returned.reshape(expert_total * capacity, width), slot_index, axis=0).reshape(
        row_count, top_count, width
    )
    expert_sum = jnp.sum(picked.astype(jnp.float32) * route_weights[:, :, None], axis=1)
    hidden_out = (residual + expert_sum).astype(jnp.bfloat16)
    return (hidden_out, new_cache)


def solution(mesh):
    in_specs = (
        P("seq", None),
        P("seq"),
        P("seq", "tp", None),
        P(),
        P(None, "tp", None),
        P("tp", None, None),
        P(),
        P("seq", None, None),
        P("seq", None, None),
        P(("seq", "tp"), None),
        P(("seq", "tp"), None),
    )
    out_specs = (P(("seq", "tp"), None), P("seq", "tp", None))
    return jax.shard_map(body, mesh=mesh, in_specs=in_specs, out_specs=out_specs, check_vma=False)
```

profile of v0, /device:TPU:0, one launch (start us, length us, event | category | flops | bytes accessed | tf_op | source)
XLA Modules:
  0.0 427.0 jit_solution(11632312372525790544)
XLA Ops:
  8.9 2.0 fusion.51
  12.4 24.7 %all-gather = bf16[16,1,512]{2,1,0:T(2,128)(2,1)S(1)} all-gather(bf16[1,1,512]{2,1,0:T(2,128)(2,1)S(1)} %reshape.295), channel_id=1, replica_groups=mesh['seq'=16,'tp'=8] {'seq'}, dimensions={0}, use_global_device_ids=true | all-gather | bytes 17408 | tf_op jit(solution)/shard_map/all_gather | solution.py:109
  37.2 23.9 %all-gather.6.cloned.1.call-done = bf16[8192,1,128]{0,2,1:T(8,128)(2,1)} async-done(((bf16[512,1,128]{0,2,1:T(8,128)(2,1)}), bf16[8192,1,128]{0,2,1:T(8,128)(2,1)}) %all-gather.6.cloned.1.call-update) | async-done | bytes 2097168 | tf_op jit(solution)/shard_map/all_gather | solution.py:108
  61.1 3.2 copy.69
  64.3 52.6 %all-gather.4.cloned.1.call-done = bf16[16384,1,128]{2,0,1:T(8,128)(2,1)} async-done(((bf16[1024,1,128]{2,0,1:T(8,128)(2,1)}), bf16[16384,1,128]{2,0,1:T(8,128)(2,1)}) %all-gather.4.cloned.1.call-update) | async-done | bytes 4194320 | tf_op jit(solution)/shard_map/all_gather | solution.py:99
  117.0 128.4 %while.31 = (s32[]{:T(128)}, f32[512,1,2]{0,2,1:T(2,128)S(1)}, f32[512,1,2]{0,2,1:T(2,128)S(1)}, f32[512,1,2,64]{0,3,2,1:T(8,128)S(1)}, bf16[16,1024,1,128]{3,1,...) while((s32[]{:T(128)}, f32[512,1,2]{0,2,1:T(2,128)S(1)}, ...), condition=%wide.region_4.5_spmd.clone, body=%wide.region_1.4_spmd.clone.sunk | while | flops 277026816 | bytes 31391872 | solution.py:92
  118.1 2.7 bitcast_reduce_fusion.2
  120.8 3.2 fusion.86
  126.1 2.7 bitcast_reduce_fusion.2
  128.8 3.2 fusion.86
  134.1 2.7 bitcast_reduce_fusion.2
  136.9 3.2 fusion.86
  142.2 2.7 bitcast_reduce_fusion.2
  144.9 3.2 fusion.86
  150.2 2.7 bitcast_reduce_fusion.2
  152.9 3.2 fusion.86
  158.2 2.7 bitcast_reduce_fusion.2
  160.9 3.2 fusion.86
  166.2 2.7 bitcast_reduce_fusion.2
  169.0 3.2 fusion.86
  174.3 2.7 bitcast_reduce_fusion.2
  177.0 3.2 fusion.86
  182.3 2.7 bitcast_reduce_fusion.2
  185.0 3.2 fusion.86
  190.3 2.7 bitcast_reduce_fusion.2
  193.0 3.2 fusion.86
  198.3 2.7 bitcast_reduce_fusion.2
  201.1 3.2 fusion.86
  206.4 2.7 bitcast_reduce_fusion.2
  209.1 3.2 fusion.86
  214.4 2.7 bitcast_reduce_fusion.2
  217.1 3.2 fusion.86
  222.4 2.7 bitcast_reduce_fusion.2
  225.1 3.2 fusion.86
  230.4 2.7 bitcast_reduce_fusion.2
  233.2 3.2 fusion.86
  238.5 2.7 bitcast_reduce_fusion.2
  241.2 3.2 fusion.86
  245.4 45.0 %while.30 = (s32[]{:T(128)}, f32[512,1,2]{0,2,1:T(2,128)S(1)}, f32[512,1,2]{0,2,1:T(2,128)S(1)}, f32[512,1,2,64]{0,3,2,1:T(8,128)S(1)}, f32[8,1024]{1,0:T(8,128)...) while((s32[]{:T(128)}, f32[512,1,2]{0,2,1:T(2,128)S(1)}, ...), condition=%wide.region_8.9_spmd.clone, body=%wide.region_5.8_spmd.clone.sunk | while | flops 284299776 | bytes 16220285 | solution.py:92
  294.1 2.4 scatter_custom_fusion
  296.6 32.7 %reduce-scatter.2.cloned.1.call-done = bf16[64,1024]{1,0:T(8,128)(2,1)} async-done(((bf16[512,1024]{1,0:T(8,128)(2,1)}), bf16[64,1024]{1,0:T(8,128)(2,1)}) %reduce-scatter.2.cloned.1.call-update) | async-done | bytes 131088 | tf_op jit(solution)/shard_map/reduce_scatter | solution.py:122
  331.5 5.4 %gather_fusion = bf16[1024,1024]{1,0:T(8,128)(2,1)} fusion(bf16[65,1024]{1,0:T(8,128)(2,1)S(1)} %concatenate.3, s32[1024]{0:T(1024)S(1)} %fusion.62), kind=kCustom, calls=%fused_computation | custom fusion | bytes 4198400 | tf_op jit(solution)/shard_map/jit(_take)/gather | solution.py:149
  336.9 2.0 broadcast_select_fusion.1
  338.9 35.5 %all_to_all.10 = bf16[16,2,32,1024]{3,2,1,0:T(8,128)(2,1)S(1)} all-to-all(bf16[16,2,32,1024]{3,2,1,0:T(8,128)(2,1)S(1)} %broadcast_select_fusion.1), channel_id=1, replica_groups=mesh['seq'=16,'tp'=8] {'seq'}, dimensions={0} | all-to-all | bytes 4194304 | tf_op jit(solution)/shard_map/all_to_all | solution.py:152
  374.4 2.4 fusion.39
  379.7 4.4 %all-to-all-start.1 = ((bf16[16,2,32,1024]{3,2,1,0:T(8,128)(2,1)}), bf16[16,2,32,1024]{3,2,1,0:T(8,128)(2,1)}, u32[]{:S(2)}, u32[]{:S(2)}) async-start(bf16[16,2,32,1024]{3,2,1,0:T(8,128)(2,1)} %copy.55), calls=%async_computation.2 | async-start | bytes 4194304 | tf_op jit(solution)/shard_map/all_to_all | solution.py:163
  385.3 28.2 %all-to-all-done.1 = bf16[16,2,32,1024]{3,2,1,0:T(8,128)(2,1)} async-done(((bf16[16,2,32,1024]{3,2,1,0:T(8,128)(2,1)}), bf16[16,2,32,1024]{3,2,1,0:T(8,128)(2,1)}, u32[]{:S(2)}, u32[]{:S(2)}) %all-to-all-start.1) | async-done | bytes 2097184 | tf_op jit(solution)/shard_map/all_to_all | solution.py:163
  413.4 4.6 %gather_fusion.1 = bf16[512,1024]{1,0:T(8,128)(2,1)S(1)} fusion(bf16[1024,1024]{1,0:T(8,128)(2,1)} %bitcast.17, s32[1024]{0:T(1024)S(1)} %pad_clamp_fusion), kind=kCustom, calls=%fused_computation.1 | custom fusion | bytes 2099200 | tf_op jit(solution)/shard_map/jit(_take)/gather | solution.py:164
  (286 shorter events, 93.1 us)
Async XLA Ops:
  7.2 369.6 %copy-start = (bf16[2,512,1024]{2,1,0:T(8,128)(2,1)S(1)}, bf16[2,512,1024]{2,1,0:T(8,128)(2,1)}, u32[]{:S(2)}) copy-start(bf16[2,512,1024]{2,1,0:T(8,128)(2,1)} %param.23) | copy-start | bytes 6291460
  7.2 5.2 %copy-start.8 = (s32[512]{0:T(512)S(1)}, s32[512]{0:T(512)}, u32[]{:S(2)}) copy-start(s32[512]{0:T(512)} %param.16) | copy-start | bytes 6148
  7.2 53.9 %all-gather.6.cloned.1.call-start = ((), (), s32[]{:S(2)}) async-start(), calls=%async_computation.4 | async-start | bytes 2228224 | tf_op jit(solution)/shard_map/all_gather | solution.py:108
  11.6 105.4 %all-gather.4.cloned.1.call-start = ((), (), s32[]{:S(2)}) async-start(), calls=%async_computation.3 | async-start | bytes 4456448 | tf_op jit(solution)/shard_map/all_gather | solution.py:99
  12.3 317.0 %reduce-scatter.2.cloned.1.call-start = ((), (), s32[]{:S(2)}) async-start(), calls=%async_computation.5 | async-start | bytes 1179648 | tf_op jit(solution)/shard_map/reduce_scatter | solution.py:122
  120.8 3.4 copy-start.1
  128.8 3.4 copy-start.1
  136.8 3.4 copy-start.1
  144.9 3.4 copy-start.1
  152.9 3.4 copy-start.1
  160.9 3.4 copy-start.1
  168.9 3.4 copy-start.1
  177.0 3.4 copy-start.1
  185.0 3.4 copy-start.1
  193.0 3.4 copy-start.1
  201.0 3.4 copy-start.1
  209.1 3.4 copy-start.1
  217.1 3.4 copy-start.1
  225.1 3.4 copy-start.1
  233.1 3.4 copy-start.1
  241.2 3.4 copy-start.1
  245.4 45.1 %copy-start.4 = (bf16[1,128,1024]{2,1,0:T(8,128)(2,1)S(1)}, bf16[1,128,1024]{2,1,0:T(8,128)(2,1)}, u32[]{:S(2)}) copy-start(bf16[1,128,1024]{2,1,0:T(8,128)(2,1)} %param.20) | copy-start | bytes 786436
  245.4 46.6 %copy-start.5 = (s32[64,8]{0,1:T(8,128)S(1)}, s32[64,8]{0,1:T(8,128)}, u32[]{:S(2)}) copy-start(s32[64,8]{0,1:T(8,128)} %param.24) | copy-start | bytes 6148
  245.4 85.0 %copy-start.6 = (f32[1024]{0:T(1024)S(1)}, f32[1024]{0:T(1024)}, u32[]{:S(2)}) copy-start(f32[1024]{0:T(1024)} %param.21) | copy-start | bytes 12292
  336.9 37.5 %copy-start.9 = (bf16[2,1024,1024]{2,1,0:T(8,128)(2,1)S(1)}, bf16[2,1024,1024]{2,1,0:T(8,128)(2,1)}, u32[]{:S(2)}) copy-start(bf16[2,1024,1024]{2,1,0:T(8,128)(2,1)} %param.22) | copy-start | bytes 12582916
  378.1 6.1 %copy-start.3 = (bf16[512,1,128]{0,2,1:T(8,128)(2,1)S(1)}, bf16[512,1,128]{0,2,1:T(8,128)(2,1)}, u32[]{:S(2)}) copy-start(bf16[512,1,128]{0,2,1:T(8,128)(2,1)} %get-tuple-element.246) | copy-start | bytes 393220
  378.1 7.1 %copy-start.7 = (f32[64,8]{0,1:T(8,128)S(1)}, f32[64,8]{0,1:T(8,128)}, u32[]{:S(2)}) copy-start(f32[64,8]{0,1:T(8,128)} %param.25) | copy-start | bytes 6148
  379.7 33.7 %all-to-all-start.1 = ((bf16[16,2,32,1024]{3,2,1,0:T(8,128)(2,1)}), bf16[16,2,32,1024]{3,2,1,0:T(8,128)(2,1)}, u32[]{:S(2)}, u32[]{:S(2)}) async-start(bf16[16,2,32,1024]{3,2,1,0:T(8,128)(2,1)} %copy.55), calls=%async_computation.2 | async-start | bytes 4194304 | tf_op jit(solution)/shard_map/all_to_all | solution.py:163
  413.4 5.4 %copy-start.2 = (bf16[64,1024]{1,0:T(8,128)(2,1)S(1)}, bf16[64,1024]{1,0:T(8,128)(2,1)}, u32[]{:S(2)}) copy-start(bf16[64,1024]{1,0:T(8,128)(2,1)} %reduce-scatter.2.cloned.1.call-done) | copy-start | bytes 393220
Sparse Core Ops, SparseCore 0:
  11.7 49.3 all-gather.5
  63.6 53.3 all-gather.3
  292.0 37.2 reduce-scatter.1
where the time goes:
time: 429 us; the launch traced here: 427 us
  waiting for transfers between devices  138 us (32%)
  matrix products  121 us (28%)
  blocking collectives  60.2 us (14%)
  local copies, waits for them, and re-layouts  49.1 us (11%)
  other arithmetic  38.4 us (9%)
  between operations  14.1 us (3%)
  starting transfers between devices  4.54 us (1%)
    dot_general x24, matrix products, attend(): jnp.einsum('tkgs,skd->tkgd', weights.astype(jnp.bfloat16), value_part, pr...  63.2 us
    all_gather x1, waiting for transfers between devices, body(): shard_piece = lax.all_gather(prefix_cache, 'seq', axis=0, tiled=True)  52.6 us
    dot_general x24, matrix products, attend(): jnp.einsum('tkgd,skd->tkgs', queries, key_part, preferred_element_type=jn...  51 us
    all_to_all x1, blocking collectives, body(): lax.all_to_all(outgoing, 'seq', split_axis=0, concat_axis=0, tiled=True)  35.5 us
    reduce_scatter x1, waiting for transfers between devices, body(): lax.psum_scatter(jnp.dot(flat_attn, flat_out, preferred_element_type=jnp....  32.7 us
    all_to_all x1, waiting for transfers between devices, body(): lax.all_to_all(answered, 'seq', split_axis=0, concat_axis=0, tiled=True)  28.2 us
    all_gather x1, blocking collectives, body(): seg_piece = lax.all_gather(seg_wire, 'seq', axis=0, tiled=True)  24.7 us
    all_gather x1, waiting for transfers between devices, body(): cache_piece = lax.all_gather(new_cache, 'seq', axis=0, tiled=True)  23.9 us
  transfers between devices with their start and end apart: 4, of which 4 were waited for; matrix products, arithmetic and copies ran while one was open for 2% of the time, Pallas kernels for 0%

commit v1 on v0

v1 whole, which is shorter than its diff:
```python
import functools

import jax
import jax.numpy as jnp
from jax import lax
from jax.experimental import pallas as pl
from jax.experimental.pallas import tpu as pltpu
from jax.sharding import PartitionSpec as P

SCALE = 0.015625
EPS = 1e-06
HD = 64
NV = 80
TD = 512
PRE = 1024
ROWS = 64
TQ = 512
NQ = 2 * TD
SEG_AT = PRE + TD
GATE_AT = SEG_AT + 16
PAY = GATE_AT + ROWS
LIMIT = 60.0
NEG = -1e30
NT = (((1,), (1,)), ((), ()))
F32 = jnp.float32
BF = jnp.bfloat16


def seq_perm(move):
    return [
        (x * 8 + y * 2 + c, (lambda t: t[0] * 8 + t[1] * 2 + t[2])(move(x, y, c)))
        for x in range(2)
        for y in range(4)
        for c in range(2)
    ]


def tp_perm(move):
    return [(q * 4 + z, (lambda t: t[0] * 4 + t[1])(move(q, z))) for q in range(2) for z in range(4)]


CORE = seq_perm(lambda x, y, c: (x, y, 1 - c))
SHIFTS = [(0, 1), (0, 3), (1, 0), (0, 2), (1, 1), (1, 3), (1, 2)]
CHIP_GROUPS = [[x * 8 + y * 2 + c for x in range(2) for y in range(4)] for c in range(2)]


def rms(wide, gain):
    mean_square = jnp.mean(wide * wide, axis=-1, keepdims=True)
    return wide * lax.rsqrt(mean_square + EPS) * gain


def project_kernel(tok_ref, gain_ref, w_ref, pre_ref, seg_ref, gate_ref, pay_ref, q_ref, new_ref):
    normed = rms(tok_ref[...].astype(F32), gain_ref[...]).astype(BF)
    proj = jnp.dot(normed, w_ref[...], preferred_element_type=F32)
    pq = proj[:, :128].astype(BF).astype(F32) * SCALE
    low = lax.broadcasted_iota(jnp.int32, (TD, 128), 1) < HD
    q_ref[:TD, :] = jnp.where(low, pq, 0.0).astype(BF)
    q_ref[TD:, :] = jnp.where(low, pltpu.roll(pq, HD, 1), 0.0).astype(BF)
    new = proj[:, 128:].astype(BF)
    new_ref[...] = new
    pay_ref[:PRE, :] = pre_ref[...]
    pay_ref[PRE:SEG_AT, :] = new
    pay_ref[SEG_AT:GATE_AT, :] = seg_ref[...]
    pay_ref[GATE_AT:, :] = gate_ref[...]


def values_t(kv):
    row = lax.broadcasted_iota(jnp.int32, (NV, 128), 0)
    col = lax.broadcasted_iota(jnp.int32, (NV, 128), 1)
    pick = jnp.where((col == row + HD) & (row < HD), 1.0, 0.0).astype(BF)
    vt = lax.dot_general(pick, kv, NT, preferred_element_type=F32)
    ones = lax.broadcasted_iota(jnp.int32, vt.shape, 0) >= HD
    return jnp.where(ones, 1.0, vt).astype(BF)


def online_step(q, kv, o_ref, m_ref, cols, mask):
    s = lax.dot_general(kv, q, NT, preferred_element_type=F32)
    if mask is not None:
        s = jnp.where(mask, s, NEG)
    m0 = m_ref[0:1, cols]
    m1 = jnp.maximum(m0, jnp.max(s, axis=0, keepdims=True))
    p = jnp.exp(s - m1).astype(BF)
    o_ref[:, cols] = o_ref[:, cols] * jnp.exp(m0 - m1) + jnp.dot(
        values_t(kv), p, preferred_element_type=F32
    )
    m_ref[0:1, cols] = m1


def prefix_kernel(*refs, count, first):
    q_ref = refs[0]
    at = 1
    if not first:
        o_in, m_in = refs[1:3]
        at = 3
    pays = refs[at : at + count]
    o_ref, m_ref, buf, top, sem = refs[at + count :]
    for j in range(count):
        pltpu.make_async_copy(pays[j].at[pl.ds(0, PRE), :], buf.at[j], sem.at[j]).start()

    def wait(j):
        pltpu.make_async_copy(pays[0].at[pl.ds(0, PRE), :], buf.at[j], sem.at[j]).wait()

    def begin():
        if first:
            o_ref[...] = jnp.zeros_like(o_ref)
        else:
            o_ref[...] = o_in[...]
            m_ref[...] = m_in[...]

    begin()
    if first:
        wait(0)
        s = lax.dot_general(buf[0, :256, :], q_ref[...], NT, preferred_element_type=F32)
        m_ref[...] = jnp.broadcast_to(jnp.max(s, axis=0, keepdims=True), m_ref.shape)
    top[...] = jnp.full_like(top, NEG)

    def block(j, _):
        if first:
            pl.when(j > 0)(lambda: wait(j))
        else:
            wait(j)
        kv = buf[j]
        vt = values_t(kv)
        for t in range(NQ // TQ):
            cols = pl.ds(t * TQ, TQ)
            s = lax.dot_general(kv, q_ref[cols, :], NT, preferred_element_type=F32)
            top[0:1, cols] = jnp.maximum(top[0:1, cols], jnp.max(s, axis=0, keepdims=True))
            p = jnp.exp(s - m_ref[0:1, cols]).astype(BF)
            o_ref[:, cols] = o_ref[:, cols] + jnp.dot(vt, p, preferred_element_type=F32)
        return 0

    lax.fori_loop(0, count, block, 0)

    @pl.when(jnp.max(top[0:1, :] - m_ref[0:1, :]) > LIMIT)
    def _():
        begin()

        def again(i, _):
            kv = buf[i // 4, pl.ds(pl.multiple_of(i % 4 * 256, 256), 256), :]
            for t in range(NQ // 256):
                cols = pl.ds(t * 256, 256)
                online_step(q_ref[cols, :], kv, o_ref, m_ref, cols, None)
            return 0

        lax.fori_loop(0, count * 4, again, 0)


def prefix_call(q, state, pays):
    count = len(pays)
    first = state is None
    vm = pl.BlockSpec(memory_space=pltpu.VMEM)
    hbm = pl.BlockSpec(memory_space=pl.ANY)
    args = (q,) + (() if first else tuple(state)) + tuple(pays)
    return pl.pallas_call(
        functools.partial(prefix_kernel, count=count, first=first),
        in_specs=[vm] * (1 if first else 3) + [hbm] * count,
        out_specs=[vm, vm],
        out_shape=[jax.ShapeDtypeStruct((NV, NQ), F32), jax.ShapeDtypeStruct((8, NQ), F32)],
        scratch_shapes=[
            pltpu.VMEM((count, PRE, 128), BF),
            pltpu.VMEM((8, NQ), F32),
            pltpu.SemaphoreType.DMA((count,)),
        ],
        cost_estimate=pl.CostEstimate(
            flops=count * PRE * NQ * 2 * 600,
            bytes_accessed=count * PRE * 256 + NQ * 256 + NV * NQ * 8,
            transcendentals=count * PRE * NQ,
        ),
        name="prefix_attention",
    )(*args)


def suffix_kernel(src_ref, q_ref, o_in, m_in, qseg_ref, start_ref, *refs):
    pays = refs[:16]
    out_ref, o_ref, m_ref, buf, segs, top, sem = refs[16:]
    own = src_ref[0]
    for j in range(16):
        at = pl.multiple_of(src_ref[j] * TD, TD)
        pltpu.make_async_copy(pays[j].at[pl.ds(PRE, TD), :], buf.at[pl.ds(at, TD), :], sem.at[0, j]).start()
        pltpu.make_async_copy(pays[j].at[pl.ds(SEG_AT, 16), :], segs.at[j], sem.at[1, j]).start()
    for j in range(16):
        pltpu.make_async_copy(pays[j].at[pl.ds(SEG_AT, 16), :], segs.at[j], sem.at[1, j]).wait()
    mine = jnp.max(jnp.where(lax.broadcasted_iota(jnp.int32, (1, NQ), 1) == 0, qseg_ref[...], -1.0))
    count = jnp.zeros((16, 128), F32)
    for j in range(16):
        same = (segs[j].astype(F32) == mine) & (src_ref[j] < own)
        count = count + jnp.where(same, 1.0, 0.0)
    back = jnp.sum(count).astype(jnp.int32)
    begin_at = own * TD - back
    start = jnp.where(qseg_ref[...] == mine, begin_at, start_ref[...] + own * TD)
    for j in range(16):
        at = pl.multiple_of(src_ref[j] * TD, TD)
        pltpu.make_async_copy(pays[j].at[pl.ds(PRE, TD), :], buf.at[pl.ds(at, TD), :], sem.at[0, j]).wait()
    lane = lax.broadcasted_iota(jnp.int32, (1, NQ), 1)
    last = own * TD + jnp.where(lane >= TD, lane - TD, lane)
    o_ref[...] = o_in[...]
    m_ref[...] = m_in[...]
    top[...] = jnp.full_like(top, NEG)
    low = begin_at // TD

    def mask_of(at, size, cols, width):
        key = at + lax.broadcasted_iota(jnp.int32, (size, width), 0)
        return (key >= cols[0]) & (key <= cols[1])

    def block(b, _):
        at = pl.multiple_of(b * TD, TD)
        kv = buf[pl.ds(at, TD), :]
        vt = values_t(kv)
        for t in range(2):
            cols = pl.ds(t * TD, TD)
            s = lax.dot_general(kv, q_ref[cols, :], NT, preferred_element_type=F32)
            span = (start[:, t * TD : t * TD + TD], last[:, t * TD : t * TD + TD])
            s = jnp.where(mask_of(at, TD, span, TD), s, NEG)
            top[0:1, cols] = jnp.maximum(top[0:1, cols], jnp.max(s, axis=0, keepdims=True))
            p = jnp.exp(s - m_ref[0:1, cols]).astype(BF)
            o_ref[:, cols] = o_ref[:, cols] + jnp.dot(vt, p, preferred_element_type=F32)
        return 0

    lax.fori_loop(low, own + 1, block, 0)

    @pl.when(jnp.max(top[0:1, :] - m_ref[0:1, :]) > LIMIT)
    def _():
        o_ref[...] = o_in[...]
        m_ref[...] = m_in[...]

        def again(i, _):
            at = pl.multiple_of(i * 256, 256)
            kv = buf[pl.ds(at, 256), :]
            for t in range(4):
                cols = pl.ds(t * 256, 256)
                span = (start[:, t * 256 : t * 256 + 256], last[:, t * 256 : t * 256 + 256])
                online_step(q_ref[cols, :], kv, o_ref, m_ref, cols, mask_of(at, 256, span, 256))
            return 0

        lax.fori_loop(low * 2, own * 2 + 2, again, 0)

    total = o_ref[...]
    mixed = total[:HD, :] / total[HD : HD + 1, :]
    both = jnp.concatenate([mixed[:, :TD], mixed[:, TD:]], axis=0)
    out_ref[...] = jnp.transpose(both).astype(BF)


def suffix_call(src, q, state, qseg, start, pays):
    vm = pl.BlockSpec(memory_space=pltpu.VMEM)
    hbm = pl.BlockSpec(memory_space=pl.ANY)
    sm = pl.BlockSpec(memory_space=pltpu.SMEM)
    return pl.pallas_call(
        suffix_kernel,
        in_specs=[sm] + [vm] * 5 + [hbm] * 16,
        out_specs=vm,
        out_shape=jax.ShapeDtypeStruct((TD, 128), BF),
        scratch_shapes=[
            pltpu.VMEM((NV, NQ), F32),
            pltpu.VMEM((8, NQ), F32),
            pltpu.VMEM((16 * TD, 128), BF),
            pltpu.VMEM((16, 16, 128), BF),
            pltpu.VMEM((8, NQ), F32),
            pltpu.SemaphoreType.DMA((2, 16)),
        ],
        cost_estimate=pl.CostEstimate(
            flops=6 * TD * NQ * 2 * 600, bytes_accessed=16 * TD * 256, transcendentals=6 * TD * NQ
        ),
        name="suffix_attention",
    )(src, q, state[0], state[1], qseg, start, *pays)


def mix_kernel(order_ref, att_ref, tok_ref, gain_ref, w0, w1, w2, w3, w4, res_ref, xi_ref):
    total = tok_ref[...].astype(F32)
    parts = [w0.at[0], w1.at[0]] + [w.at[i] for w in (w2, w3, w4) for i in range(2)]
    acc = jnp.zeros((ROWS, 1024), F32)
    for j in range(8):
        acc = acc + jnp.dot(att_ref[order_ref[j + 1]], parts[j][...], preferred_element_type=F32)
    total = total + acc
    res_ref[...] = total
    xi_ref[...] = rms(total, gain_ref[...]).astype(BF)


def mix_call(order, att, tokens, gain, ws):
    def full(a):
        zeros = (0,) * a.ndim
        return pl.BlockSpec(a.shape, lambda i, o: zeros)

    out = pl.BlockSpec((ROWS, 1024), lambda i, o: (0, 0))
    return pl.pallas_call(
        mix_kernel,
        grid_spec=pltpu.PrefetchScalarGridSpec(
            num_scalar_prefetch=1,
            grid=(1,),
            in_specs=[full(att), pl.BlockSpec((ROWS, 1024), lambda i, o: (o[0], 0)), full(gain)]
            + [full(w) for w in ws],
            out_specs=[out, out],
        ),
        out_shape=[
            jax.ShapeDtypeStruct((ROWS, 1024), F32),
            jax.ShapeDtypeStruct((ROWS, 1024), BF),
        ],
        name="mix",
    )(order, att, tokens, gain, *ws)


def expert_kernel(num_ref, x_ref, wi_own, wi_peer, wo_own, wo_peer, *refs):
    gates = refs[:8]
    out_ref, acc, table = refs[8:]
    e = pl.program_id(0)

    @pl.when(e == 0)
    def _():
        for j in range(8):
            at = pl.multiple_of(num_ref[4 + j] * ROWS, ROWS)
            table[pl.ds(at, ROWS), :] = gates[j][...].astype(F32)

    def run(wi, wo, add):
        x = x_ref[...]
        joined = jnp.dot(x, wi[0], preferred_element_type=F32)
        g = joined[:, :512]
        hidden = (g / (1.0 + jnp.exp(-g)) * joined[:, 512:]).astype(BF)
        o = jnp.dot(hidden, wo[0], preferred_element_type=F32).astype(BF).astype(F32)
        lane = lax.broadcasted_iota(jnp.int32, (512, 128), 1)
        number = num_ref[e]
        hit = (lane == number) | (lane == number + 32)
        gate = jnp.sum(jnp.where(hit, table[...], 0.0), axis=1, keepdims=True)
        o = o * gate
        if add:
            acc[...] = acc[...] + o
        else:
            acc[...] = o

    pl.when(e == 0)(lambda: run(wi_own, wo_own, False))
    pl.when(e == 1)(lambda: run(wi_own, wo_own, True))
    pl.when(e >= 2)(lambda: run(wi_peer, wo_peer, True))

    @pl.when(e == 3)
    def _():
        out_ref[...] = acc[...].astype(BF)


def expert_call(numbers, x, wi_own, wi_peer, wo_own, wo_peer, pays):
    own = lambda e, n: (jnp.minimum(e, 1), 0, 0)
    peer = lambda e, n: (jnp.maximum(e - 2, 0), 0, 0)
    fixed = lambda e, n: (0, 0)
    return pl.pallas_call(
        expert_kernel,
        grid_spec=pltpu.PrefetchScalarGridSpec(
            num_scalar_prefetch=1,
            grid=(4,),
            in_specs=[
                pl.BlockSpec((512, 1024), fixed),
                pl.BlockSpec((1, 1024, 1024), own),
                pl.BlockSpec((1, 1024, 1024), peer),
                pl.BlockSpec((1, 512, 1024), own),
                pl.BlockSpec((1, 512, 1024), peer),
            ]
            + [pl.BlockSpec((ROWS, 128), fixed)] * 8,
            out_specs=pl.BlockSpec((512, 1024), fixed),
            scratch_shapes=[pltpu.VMEM((512, 1024), F32), pltpu.VMEM((512, 128), F32)],
        ),
        out_shape=jax.ShapeDtypeStruct((512, 1024), BF),
        name="experts",
    )(numbers, x, wi_own, wi_peer, wo_own, wo_peer, *pays)


def body(
    tokens,
    segment_ids,
    prefix_cache,
    norm1_gain,
    w_qkv,
    w_out,
    norm2_gain,
    expert_in,
    expert_out,
    routes,
    route_weights,
):
    seq = lax.axis_index("seq")
    tp = lax.axis_index("tp")
    x, y, c = seq // 8, seq // 2 % 4, seq % 2
    q4, z = tp // 4, tp % 4

    segf = segment_ids.astype(F32)
    seg_rows = jnp.concatenate([segf.reshape(4, 128), jnp.full((12, 128), -1.0, F32)]).astype(BF)
    local = jnp.sum((segment_ids[:, None] < segment_ids[None, :]).astype(jnp.int32), axis=0)
    start = jnp.concatenate([local, local])[None, :]
    qseg = jnp.concatenate([segf, segf])[None, :]
    dense = jnp.sum(
        jnp.where(
            routes[:, :, None] == jnp.arange(32, dtype=jnp.int32), route_weights[:, :, None], 0.0
        ),
        axis=1,
    )
    high = lax.reduce_precision(dense, 8, 7)
    gates = jnp.concatenate([high, dense - high, jnp.zeros((ROWS, 64), F32)], axis=1).astype(BF)

    pay, q, new = pl.pallas_call(
        project_kernel,
        out_shape=[
            jax.ShapeDtypeStruct((PAY, 128), BF),
            jax.ShapeDtypeStruct((NQ, 128), BF),
            jax.ShapeDtypeStruct((TD, 128), BF),
        ],
        name="project",
    )(
        tokens,
        norm1_gain[None, :],
        w_qkv.reshape(1024, 256),
        prefix_cache.reshape(PRE, 128),
        seg_rows,
        gates,
    )

    far = [
        lax.ppermute(
            pay, "seq", seq_perm(lambda a, b, d, i=i, j=j: ((a + i) % 2, (b + j) % 4, d))
        )
        for i, j in SHIFTS
    ]
    wi_peer = lax.ppermute(expert_in, "seq", CORE)
    wo_peer = lax.ppermute(expert_out, "seq", CORE)
    near = [lax.ppermute(p, "seq", CORE) for p in [pay] + far]
    wx = lax.ppermute(w_out, "tp", tp_perm(lambda a, b: (1 - a, b)))
    wpair = jnp.concatenate([w_out, wx])
    wz = [lax.ppermute(wpair, "tp", tp_perm(lambda a, b, k=k: (a, (b + k) % 4))) for k in (1, 3, 2)]

    state = prefix_call(q, None, [pay, near[0]])
    state = prefix_call(q, state, [p for k in range(3) for p in (far[k], near[k + 1])])
    state = prefix_call(q, state, [p for k in range(3, 7) for p in (far[k], near[k + 1])])
    chips = [(x, y)] + [((x - i) % 2, (y - j) % 4) for i, j in SHIFTS]
    same = [a * 8 + b * 2 + c for a, b in chips]
    other = [a * 8 + b * 2 + (1 - c) for a, b in chips]
    src = jnp.stack([v for pair in zip(same, other) for v in pair]).astype(jnp.int32)
    pays = [v for pair in zip([pay] + far, near) for v in pair]
    attended = suffix_call(src, q, state, qseg, start, pays)

    spread = lax.all_to_all(attended.reshape(8, ROWS, 128), "tp", 0, 0, tiled=True)
    heads = [q4 * 4 + z, (1 - q4) * 4 + z]
    for k in (1, 3, 2):
        heads += [q4 * 4 + (z - k) % 4, (1 - q4) * 4 + (z - k) % 4]
    order = jnp.stack([tp] + heads).astype(jnp.int32)
    residual, xi = mix_call(order, spread, tokens, norm2_gain[None, :], [w_out, wx] + wz)

    everyone = lax.all_to_all(
        jnp.broadcast_to(xi[None], (8, ROWS, 1024)),
        "seq",
        0,
        0,
        axis_index_groups=CHIP_GROUPS,
        tiled=True,
    )
    peer = x * 8 + y * 2 + (1 - c)
    numbers = jnp.stack(
        [seq * 2, seq * 2 + 1, peer * 2, peer * 2 + 1] + [a * 4 + b for a, b in chips]
    ).astype(jnp.int32)
    gate_parts = [p[GATE_AT:] for p in [pay] + far]
    partial = expert_call(
        numbers, everyone.reshape(512, 1024), expert_in, wi_peer, expert_out, wo_peer, gate_parts
    )
    returned = lax.all_to_all(
        partial.reshape(8, ROWS, 1024), "seq", 0, 0, axis_index_groups=CHIP_GROUPS, tiled=True
    )
    hidden = (residual + jnp.sum(returned.astype(F32), axis=0)).astype(BF)
    return hidden, new.reshape(TD, 1, 128)


def solution(mesh):
    in_specs = (
        P("seq", None),
        P("seq"),
        P("seq", "tp", None),
        P(),
        P(None, "tp", None),
        P("tp", None, None),
        P(),
        P("seq", None, None),
        P("seq", None, None),
        P(("seq", "tp"), None),
        P(("seq", "tp"), None),
    )
    out_specs = (P(("seq", "tp"), None), P("seq", "tp", None))
    return jax.shard_map(body, mesh=mesh, in_specs=in_specs, out_specs=out_specs, check_vma=False)
```

time: 429 us -> 250 us (0.58)
  matrix products: 121 us -> 0 us
  Pallas kernels: 0 us -> 119 us
  waiting for transfers between devices: 138 us -> 43.1 us
  blocking collectives: 60.2 us -> 20 us
  starting transfers between devices: 4.54 us -> 42.1 us
  other arithmetic: 38.4 us -> 4.4 us
  local copies, waits for them, and re-layouts: 49.1 us -> 18.5 us
  between operations: 14.1 us -> 0.83 us
    dot_general x52 -> x0, matrix products: 121 us -> none  [the longest x24 63.2 us: attend(): jnp.einsum('tkgs,skd->tkgd', weights.astype(jnp.bfloat16), value_part, pr...]
    pallas_call x0 -> x7, Pallas kernels: none -> 119 us  [the longest x3 94.7 us: prefix_call(): pl.pallas_call(functools.partial(prefix_kernel, count=count, first=first)...]
    all_gather x2 -> x0, waiting for transfers between devices: 76.5 us -> none  [the longest x1 52.6 us: body(): shard_piece = lax.all_gather(prefix_cache, 'seq', axis=0, tiled=True)]
    ppermute x0 -> x21, waiting for transfers between devices: none -> 35.4 us  [the longest x7 28.2 us: body(): lax.ppermute(pay, 'seq', seq_perm(lambda a, b, d, i=i, j=j: ((a + i) % 2,...]
    reduce_scatter x1 -> x0, waiting for transfers between devices: 32.7 us -> none  [body(): lax.psum_scatter(jnp.dot(flat_attn, flat_out, preferred_element_type=jnp....]
    all_gather x1 -> x0, blocking collectives: 24.7 us -> none  [body(): seg_piece = lax.all_gather(seg_wire, 'seq', axis=0, tiled=True)]
    ppermute x0 -> x21, starting transfers between devices: none -> 23.8 us  [the longest x7 14.7 us: body(): lax.ppermute(pay, 'seq', seq_perm(lambda a, b, d, i=i, j=j: ((a + i) % 2,...]
    reduce_sum x28 -> x3, other arithmetic: 23.7 us -> 1.13 us  [the longest x1 0.77 us: body(): jnp.sum(jnp.where(routes[:, :, None] == jnp.arange(32, dtype=jnp.int32),...]
  transfers between devices with their start and end apart: 4 -> 23, of which waited for: 4 -> 7; matrix products, arithmetic and copies ran while one was open for 2% -> 7% of each run, Pallas kernels for 0% -> 42%
where the time goes in v1:
time: 250 us; the launch traced here: 248 us
  Pallas kernels  119 us (48%)
  waiting for transfers between devices  43.1 us (17%)
  starting transfers between devices  42.1 us (17%)
  blocking collectives  20 us (8%)
  local copies, waits for them, and re-layouts  18.5 us (7%)
  other arithmetic  4.4 us (2%)
    pallas_call x3, Pallas kernels, prefix_call(): pl.pallas_call(functools.partial(prefix_kernel, count=count, first=first)...  94.7 us
    ppermute x7, waiting for transfers between devices, body(): lax.ppermute(pay, 'seq', seq_perm(lambda a, b, d, i=i, j=j: ((a + i) % 2,...  28.2 us
    all_to_all x1, blocking collectives, body(): lax.all_to_all(partial.reshape(8, ROWS, 1024), 'seq', 0, 0, axis_index_gr...  20 us
    ppermute x7, starting transfers between devices, body(): lax.ppermute(pay, 'seq', seq_perm(lambda a, b, d, i=i, j=j: ((a + i) % 2,...  14.7 us
    all_to_all x1, starting transfers between devices, body(): lax.all_to_all(jnp.broadcast_to(xi[None], (8, ROWS, 1024)), 'seq', 0, 0,...  14.6 us
    pallas_call x1, Pallas kernels, expert_call(): pl.pallas_call(expert_kernel, grid_spec=pltpu.PrefetchScalarGridSpec(num_...  12.8 us
    slice x8, local copies, waits for them, and re-layouts, body(): gate_parts = [p[GATE_AT:] for p in [pay] + far]  10.5 us
    ppermute x1, waiting for transfers between devices, body(): wx = lax.ppermute(w_out, 'tp', tp_perm(lambda a, b: (1 - a, b)))  7.15 us
  transfers between devices with their start and end apart: 23, of which 7 were waited for; matrix products, arithmetic and copies ran while one was open for 7% of the time, Pallas kernels for 42%

profile of v1, /device:TPU:0, one launch (start us, length us, event | category | flops | bytes accessed | tf_op | source)
XLA Modules:
  0.0 248.1 jit_solution(10486300485442302266)
XLA Ops:
  0.7 0.8 select_reduce_fusion
  1.6 0.7 fusion.1
  3.0 0.7 maximum_maximum_fusion.gate_ref
  3.7 3.0 %project.1 = (bf16[1616,128]{1,0:T(8,128)(2,1)}, bf16[1024,128]{1,0:T(8,128)(2,1)}, bf16[512,128]{1,0:T(8,128)(2,1)}) custom-call(bf16[512,1024]{1,0:T(8,128)(2,1)} %tok_ref.3, f32[1,1024]{1,0:T(1,128)} %bitcast.54, bf16[1024,256]{1,0:T(8,128)(2,1)} %bitcast.51, bf16[1024,128]{1,0:T(8,128)(2,1)} %bitcast.52, bf16[16,128]{1,0:T(8,128)(2,1)} %concatenate.16.seg_ref, ...), custom_call_target="tpu_custom_call" | custom-call | tf_op jit(solution)/shard_map/project/pallas_call | solution.py:394
  6.6 1.7 collective-permute-start.1
  8.3 1.6 collective-permute-start.3
  10.0 1.5 collective-permute-start.15
  11.5 7.2 %collective-permute-done.15.w1 = bf16[1,128,1024]{2,1,0:T(8,128)(2,1)S(1)} collective-permute-done((bf16[1,128,1024]{2,1,0:T(8,128)(2,1)S(1)}, bf16[1,128,1024]{2,1,0:T(8,128)(2,1)S(1)}, u32[]{:S(2)}, u32[]{:S(2)}) %collective-permute-start.15) | collective-permute-done | bytes 262176 | tf_op jit(solution)/shard_map/ppermute | solution.py:420
  18.6 3.1 %collective-permute-start.5 = (bf16[1616,128]{1,0:T(8,128)(2,1)}, bf16[1616,128]{1,0:T(8,128)(2,1)S(1)}, u32[]{:S(2)}, u32[]{:S(2)}) collective-permute-start(bf16[1616,128]{1,0:T(8,128)(2,1)} %get-tuple-element.14.refs_1_.refs_0_), channel_id=1, source_target_pairs={{0,64},{8,72},{16,80},{24,88},{32,96},{40,104},{48,112},{56,120},{... | collective-permute-start | bytes 1241096 | tf_op jit(solution)/shard_map/ppermute | solution.py:412
  22.0 5.3 %collective-permute-start.11 = (bf16[1616,128]{1,0:T(8,128)(2,1)}, bf16[1616,128]{1,0:T(8,128)(2,1)}, u32[]{:S(2)}, u32[]{:S(2)}) collective-permute-start(bf16[1616,128]{1,0:T(8,128)(2,1)} %get-tuple-element.14.refs_1_.refs_0_), channel_id=1, source_target_pairs={{0,112},{8,120},{16,64},{24,72},{32,80},{40,88},{48,96},{56,104},{... | collective-permute-start | bytes 1241096 | tf_op jit(solution)/shard_map/ppermute | solution.py:412
  27.4 0.7 collective-permute-start.13
  28.1 0.6 stack.146.src_ref
  29.3 0.7 constant_dynamic-update-slice_fusion.1
  30.2 2.6 %collective-permute-done.5.refs_7_.refs_6_ = bf16[1616,128]{1,0:T(8,128)(2,1)S(1)} collective-permute-done((bf16[1616,128]{1,0:T(8,128)(2,1)}, bf16[1616,128]{1,0:T(8,128)(2,1)S(1)}, u32[]{:S(2)}, u32[]{:S(2)}) %collective-permute-start.5) | collective-permute-done | bytes 413728 | tf_op jit(solution)/shard_map/ppermute | solution.py:412
  32.8 2.0 collective-permute-start.7
  34.8 8.2 %collective-permute-done.9.refs_5_.refs_10_ = bf16[1616,128]{1,0:T(8,128)(2,1)S(1)} collective-permute-done((bf16[1616,128]{1,0:T(8,128)(2,1)}, bf16[1616,128]{1,0:T(8,128)(2,1)S(1)}, u32[]{:S(2)}, u32[]{:S(2)}) %collective-permute-start.9) | collective-permute-done | bytes 413728 | tf_op jit(solution)/shard_map/ppermute | solution.py:412
  43.0 7.6 %collective-permute-done.11.refs_7_.refs_12_ = bf16[1616,128]{1,0:T(8,128)(2,1)} collective-permute-done((bf16[1616,128]{1,0:T(8,128)(2,1)}, bf16[1616,128]{1,0:T(8,128)(2,1)}, u32[]{:S(2)}, u32[]{:S(2)}) %collective-permute-start.11) | collective-permute-done | bytes 413728 | tf_op jit(solution)/shard_map/ppermute | solution.py:412
  50.6 9.9 %collective-permute-done.13.refs_9_.refs_14_ = bf16[1616,128]{1,0:T(8,128)(2,1)} collective-permute-done((bf16[1616,128]{1,0:T(8,128)(2,1)}, bf16[1616,128]{1,0:T(8,128)(2,1)}, u32[]{:S(2)}, u32[]{:S(2)}) %collective-permute-start.13) | collective-permute-done | bytes 413728 | tf_op jit(solution)/shard_map/ppermute | solution.py:412
  61.1 0.8 constant_dynamic-update-slice_fusion
  61.9 13.8 %prefix_attention.3 = (f32[80,1024]{1,0:T(8,128)}, f32[8,1024]{1,0:T(8,128)}) custom-call(bf16[1024,128]{1,0:T(8,128)(2,1)} %get-tuple-element.13.refs_0_.q_ref, bf16[1616,128]{1,0:T(8,128)(2,1)} %get-tuple-element.14.refs_1_.refs_0_, bf16[1616,128]{1,0:T(8,128)(2,1)} %copy-done.12), custom_call_target="tpu_custom_call" | custom-call | flops 2516582400 | bytes 1441792 | tf_op jit(solution)/shard_map/prefix_attention/pallas_call | solution.py:154
  75.7 0.6 collective-permute-start.10
  77.1 35.2 %prefix_attention.4 = (f32[80,1024]{1,0:T(8,128)}, f32[8,1024]{1,0:T(8,128)}) custom-call(bf16[1024,128]{1,0:T(8,128)(2,1)} %get-tuple-element.13.refs_0_.q_ref, f32[80,1024]{1,0:T(8,128)} %get-tuple-element.15.refs_1_, f32[8,1024]{1,0:T(8,128)} %get-tuple-element.16.refs_2_, bf16[1616,128]{1,0:T(8,128)(2,1)} %copy-done.8, bf16[1616,128]{1,0:T(8,128)(2,1)} %copy-done.13, ...), custom_call_target="tpu_custom_call" | custom-call | flops 7549747200 | bytes 2490368 | tf_op jit(solution)/shard_map/prefix_attention/pallas_call | solution.py:154
  112.6 1.9 collective-permute-start.16
  114.5 1.3 collective-permute-start.17
  115.9 2.7 %collective-permute-start.18 = (bf16[2,128,1024]{2,1,0:T(8,128)(2,1)}, bf16[2,128,1024]{2,1,0:T(8,128)(2,1)}, u32[]{:S(2)}, u32[]{:S(2)}) collective-permute-start(bf16[2,128,1024]{2,1,0:T(8,128)(2,1)} %constant_dynamic-update-slice_fusion), channel_id=1, source_target_pairs={{0,2},{1,3},{2,0},{3,1},{4,6},{5,7},{6,4},{7,5},{8,10},{9,11},{10,... | collective-permute-start | bytes 1572872 | tf_op jit(solution)/shard_map/ppermute | solution.py:422
  118.5 45.7 %prefix_attention.5 = (f32[80,1024]{1,0:T(8,128)}, f32[8,1024]{1,0:T(8,128)}) custom-call(bf16[1024,128]{1,0:T(8,128)(2,1)} %get-tuple-element.13.refs_0_.q_ref, f32[80,1024]{1,0:T(8,128)} %get-tuple-element.17.refs_1_, f32[8,1024]{1,0:T(8,128)} %get-tuple-element.18.refs_2_, bf16[1616,128]{1,0:T(8,128)(2,1)} %collective-permute-done.7.refs_3_.refs_8_, ...), custom_call_target="tpu_custom_call" | custom-call | flops 10066329600 | bytes 3014656 | tf_op jit(solution)/shard_map/prefix_attention/pallas_call | solution.py:154
  164.3 5.2 %suffix_attention.1 = bf16[512,128]{1,0:T(8,128)(2,1)} custom-call(s32[16]{0:T(128)} %stack.146.src_ref, bf16[1024,128]{1,0:T(8,128)(2,1)} %get-tuple-element.13.refs_0_.q_ref, f32[80,1024]{1,0:T(8,128)} %get-tuple-element.19.o_in, f32[8,1024]{1,0:T(8,128)} %get-tuple-element.20.m_in, f32[1,1024]{1,0:T(1,128)} %bitcast.56, s32[1,1024]{1,0:T(1,128)} %bitcast.57, ...), custom_call_target="tpu_custom_call" | custom-call | flops 3774873600 | bytes 2097152 | tf_op jit(solution)/shard_map/suffix_attention/pallas_call | solution.py:247
  169.5 3.7 %all-to-all-start = ((bf16[8,64,128]{2,1,0:T(8,128)(2,1)}), bf16[8,64,128]{2,1,0:T(8,128)(2,1)S(1)}, u32[]{:S(2)}, u32[]{:S(2)}) async-start(bf16[8,64,128]{2,1,0:T(8,128)(2,1)} %bitcast.53), calls=%async_computation | async-start | bytes 262144 | tf_op jit(solution)/shard_map/all_to_all | solution.py:434
  173.2 0.6 stack.129.order_ref
  173.8 6.2 %all-to-all-done.att_ref = bf16[8,64,128]{2,1,0:T(8,128)(2,1)S(1)} async-done(((bf16[8,64,128]{2,1,0:T(8,128)(2,1)}), bf16[8,64,128]{2,1,0:T(8,128)(2,1)S(1)}, u32[]{:S(2)}, u32[]{:S(2)}) %all-to-all-start) | async-done | bytes 131104 | tf_op jit(solution)/shard_map/all_to_all | solution.py:434
  180.0 0.7 copy-done.4
  180.7 3.5 %mix.1 = (f32[64,1024]{1,0:T(8,128)}, bf16[64,1024]{1,0:T(8,128)(2,1)}) custom-call(s32[9]{0:T(128)} %stack.129.order_ref, bf16[8,64,128]{2,1,0:T(8,128)(2,1)} %copy-done.4, bf16[512,1024]{1,0:T(8,128)(2,1)} %tok_ref.3, f32[1,1024]{1,0:T(1,128)} %bitcast.55, bf16[1,128,1024]{2,1,0:T(8,128)(2,1)} %w0.1, bf16[1,128,1024]{2,1,0:T(8,128)(2,1)} %copy-done.3, ...), custom_call_target="tpu_custom_call" | custom-call | tf_op jit(solution)/shard_map/mix/pallas_call | solution.py:284
  184.2 2.0 broadcast_in_dim.46
  186.2 14.6 %all-to-all-start.1 = ((bf16[8,64,1024]{2,1,0:T(8,128)(2,1)}), bf16[8,64,1024]{2,1,0:T(8,128)(2,1)S(1)}, u32[]{:S(2)}, u32[]{:S(2)}) async-start(bf16[8,64,1024]{2,1,0:T(8,128)(2,1)} %broadcast_in_dim.46), calls=%async_computation.1 | async-start | bytes 2097152 | tf_op jit(solution)/shard_map/all_to_all | solution.py:441
  200.8 1.3 slice.24.refs_0_
  202.1 0.6 stack.159.num_ref
  202.7 1.3 slice.32.refs_1_
  204.1 1.3 slice.33.refs_2_
  205.4 1.3 slice.34.refs_3_
  206.7 1.3 slice.35.refs_4_
  208.0 1.3 slice.36.refs_5_
  209.3 1.3 slice.37.refs_6_
  210.6 1.3 slice.38.refs_7_
  212.0 1.5 all-to-all-done.1
  213.5 1.0 copy-done
  214.4 12.8 %experts.1 = bf16[512,1024]{1,0:T(8,128)(2,1)} custom-call(s32[12]{0:T(128)} %stack.159.num_ref, bf16[512,1024]{1,0:T(8,128)(2,1)} %bitcast.49, bf16[2,1024,1024]{2,1,0:T(8,128)(2,1)} %wi_own.1, bf16[2,1024,1024]{2,1,0:T(8,128)(2,1)} %collective-permute-done.19.wi_peer, bf16[2,512,1024]{2,1,0:T(8,128)(2,1)} %wo_own.1, ...), custom_call_target="tpu_custom_call" | custom-call | tf_op jit(solution)/shard_map/experts/pallas_call | solution.py:341
  227.2 20.0 %all_to_all.15 = bf16[8,64,1024]{2,1,0:T(8,128)(2,1)S(1)} all-to-all(bf16[8,64,1024]{2,1,0:T(8,128)(2,1)} %bitcast.50), channel_id=1, replica_groups={{0,16,32,48,64,80,96,112},{8,24,40,56,72,88,104,120},{1,17,33,49,65,81,..., dimensions={0} | all-to-all | bytes 2097152 | tf_op jit(solution)/shard_map/all_to_all | solution.py:457
  247.4 0.7 add_convert_fusion
  (67 shorter events, 4.0 us)
Async XLA Ops:
  0.6 29.4 %copy-start.7 = (s32[512]{0:T(512)S(1)}, s32[512]{0:T(512)}, u32[]{:S(2)}) copy-start(s32[512]{0:T(512)} %param.12) | copy-start | bytes 6148
  0.6 9.3 %copy-start.2 = (bf16[1,128,1024]{2,1,0:T(8,128)(2,1)S(1)}, bf16[1,128,1024]{2,1,0:T(8,128)(2,1)}, u32[]{:S(2)}) copy-start(bf16[1,128,1024]{2,1,0:T(8,128)(2,1)} %w0.1) | copy-start | bytes 786436
  6.6 15.1 %collective-permute-start = (bf16[1616,128]{1,0:T(8,128)(2,1)}, bf16[1616,128]{1,0:T(8,128)(2,1)S(1)}, u32[]{:S(2)}, u32[]{:S(2)}) collective-permute-start(bf16[1616,128]{1,0:T(8,128)(2,1)} %get-tuple-element.14.refs_1_.refs_0_), channel_id=1, source_target_pairs={{0,8},{8,0},{16,24},{24,16},{32,40},{40,32},{48,56},{56,48},{64,72... | collective-permute-start | bytes 1241096 | tf_op jit(solution)/shard_map/ppermute | solution.py:419
  6.6 15.4 %collective-permute-start.1 = (bf16[1616,128]{1,0:T(8,128)(2,1)}, bf16[1616,128]{1,0:T(8,128)(2,1)S(1)}, u32[]{:S(2)}, u32[]{:S(2)}) collective-permute-start(bf16[1616,128]{1,0:T(8,128)(2,1)} %get-tuple-element.14.refs_1_.refs_0_), channel_id=1, source_target_pairs={{0,16},{8,24},{16,32},{24,40},{32,48},{40,56},{48,0},{56,8},{64,80... | collective-permute-start | bytes 1241096 | tf_op jit(solution)/shard_map/ppermute | solution.py:412
  8.3 19.1 %collective-permute-start.3 = (bf16[1616,128]{1,0:T(8,128)(2,1)}, bf16[1616,128]{1,0:T(8,128)(2,1)S(1)}, u32[]{:S(2)}, u32[]{:S(2)}) collective-permute-start(bf16[1616,128]{1,0:T(8,128)(2,1)} %get-tuple-element.14.refs_1_.refs_0_), channel_id=1, source_target_pairs={{0,48},{8,56},{16,0},{24,8},{32,16},{40,24},{48,32},{56,40},{64,11... | collective-permute-start | bytes 1241096 | tf_op jit(solution)/shard_map/ppermute | solution.py:412
  9.9 203.6 %collective-permute-start.19 = (bf16[2,1024,1024]{2,1,0:T(8,128)(2,1)}, bf16[2,1024,1024]{2,1,0:T(8,128)(2,1)}, u32[]{:S(2)}, u32[]{:S(2)}) collective-permute-start(bf16[2,1024,1024]{2,1,0:T(8,128)(2,1)} %wi_own.1), channel_id=1, source_target_pairs={{0,8},{8,0},{16,24},{24,16},{32,40},{40,32},{48,56},{56,48},{64,72... | collective-permute-start | bytes 12582920 | tf_op jit(solution)/shard_map/ppermute | solution.py:417
  10.0 8.6 %collective-permute-start.15 = (bf16[1,128,1024]{2,1,0:T(8,128)(2,1)S(1)}, bf16[1,128,1024]{2,1,0:T(8,128)(2,1)S(1)}, u32[]{:S(2)}, u32[]{:S(2)}) collective-permute-start(bf16[1,128,1024]{2,1,0:T(8,128)(2,1)S(1)} %copy-done.2), channel_id=1, source_target_pairs={{0,4},{1,5},{2,6},{3,7},{4,0},{5,1},{6,2},{7,3},{8,12},{9,13},{10,... | collective-permute-start | bytes 786440 | tf_op jit(solution)/shard_map/ppermute | solution.py:420
  18.6 57.0 %copy-start.3 = (bf16[1,128,1024]{2,1,0:T(8,128)(2,1)}, bf16[1,128,1024]{2,1,0:T(8,128)(2,1)S(1)}, u32[]{:S(2)}) copy-start(bf16[1,128,1024]{2,1,0:T(8,128)(2,1)S(1)} %collective-permute-done.15.w1) | copy-start | bytes 786436
  18.6 14.2 %collective-permute-start.5 = (bf16[1616,128]{1,0:T(8,128)(2,1)}, bf16[1616,128]{1,0:T(8,128)(2,1)S(1)}, u32[]{:S(2)}, u32[]{:S(2)}) collective-permute-start(bf16[1616,128]{1,0:T(8,128)(2,1)} %get-tuple-element.14.refs_1_.refs_0_), channel_id=1, source_target_pairs={{0,64},{8,72},{16,80},{24,88},{32,96},{40,104},{48,112},{56,120},{... | collective-permute-start | bytes 1241096 | tf_op jit(solution)/shard_map/ppermute | solution.py:412
  21.7 40.2 %copy-start.12 = (bf16[1616,128]{1,0:T(8,128)(2,1)}, bf16[1616,128]{1,0:T(8,128)(2,1)S(1)}, u32[]{:S(2)}) copy-start(bf16[1616,128]{1,0:T(8,128)(2,1)S(1)} %collective-permute-done.refs_2_.refs_1_) | copy-start | bytes 1241092
  21.7 21.3 %collective-permute-start.9 = (bf16[1616,128]{1,0:T(8,128)(2,1)}, bf16[1616,128]{1,0:T(8,128)(2,1)S(1)}, u32[]{:S(2)}, u32[]{:S(2)}) collective-permute-start(bf16[1616,128]{1,0:T(8,128)(2,1)} %get-tuple-element.14.refs_1_.refs_0_), channel_id=1, source_target_pairs={{0,80},{8,88},{16,96},{24,104},{32,112},{40,120},{48,64},{56,72},{... | collective-permute-start | bytes 1241096 | tf_op jit(solution)/shard_map/ppermute | solution.py:412
  22.0 53.6 %copy-start.8 = (bf16[1616,128]{1,0:T(8,128)(2,1)}, bf16[1616,128]{1,0:T(8,128)(2,1)S(1)}, u32[]{:S(2)}) copy-start(bf16[1616,128]{1,0:T(8,128)(2,1)S(1)} %collective-permute-done.1.refs_3_.refs_2_) | copy-start | bytes 1241092
  22.0 28.6 %collective-permute-start.11 = (bf16[1616,128]{1,0:T(8,128)(2,1)}, bf16[1616,128]{1,0:T(8,128)(2,1)}, u32[]{:S(2)}, u32[]{:S(2)}) collective-permute-start(bf16[1616,128]{1,0:T(8,128)(2,1)} %get-tuple-element.14.refs_1_.refs_0_), channel_id=1, source_target_pairs={{0,112},{8,120},{16,64},{24,72},{32,80},{40,88},{48,96},{56,104},{... | collective-permute-start | bytes 1241096 | tf_op jit(solution)/shard_map/ppermute | solution.py:412
  27.4 48.3 %copy-start.9 = (bf16[1616,128]{1,0:T(8,128)(2,1)}, bf16[1616,128]{1,0:T(8,128)(2,1)S(1)}, u32[]{:S(2)}) copy-start(bf16[1616,128]{1,0:T(8,128)(2,1)S(1)} %collective-permute-done.3.refs_5_.refs_4_) | copy-start | bytes 1241092
  27.4 33.1 %collective-permute-start.13 = (bf16[1616,128]{1,0:T(8,128)(2,1)}, bf16[1616,128]{1,0:T(8,128)(2,1)}, u32[]{:S(2)}, u32[]{:S(2)}) collective-permute-start(bf16[1616,128]{1,0:T(8,128)(2,1)} %get-tuple-element.14.refs_1_.refs_0_), channel_id=1, source_target_pairs={{0,96},{8,104},{16,112},{24,120},{32,64},{40,72},{48,80},{56,88},{... | collective-permute-start | bytes 1241096 | tf_op jit(solution)/shard_map/ppermute | solution.py:412
  32.8 42.9 %copy-start.10 = (bf16[1616,128]{1,0:T(8,128)(2,1)}, bf16[1616,128]{1,0:T(8,128)(2,1)S(1)}, u32[]{:S(2)}) copy-start(bf16[1616,128]{1,0:T(8,128)(2,1)S(1)} %collective-permute-done.5.refs_7_.refs_6_) | copy-start | bytes 1241092
  32.8 42.9 %collective-permute-start.7 = (bf16[1616,128]{1,0:T(8,128)(2,1)}, bf16[1616,128]{1,0:T(8,128)(2,1)}, u32[]{:S(2)}, u32[]{:S(2)}) collective-permute-start(bf16[1616,128]{1,0:T(8,128)(2,1)} %get-tuple-element.14.refs_1_.refs_0_), channel_id=1, source_target_pairs={{0,32},{8,40},{16,48},{24,56},{32,0},{40,8},{48,16},{56,24},{64,96... | collective-permute-start | bytes 1241096 | tf_op jit(solution)/shard_map/ppermute | solution.py:412
  43.0 32.7 %copy-start.11 = (bf16[1616,128]{1,0:T(8,128)(2,1)}, bf16[1616,128]{1,0:T(8,128)(2,1)S(1)}, u32[]{:S(2)}) copy-start(bf16[1616,128]{1,0:T(8,128)(2,1)S(1)} %collective-permute-done.9.refs_5_.refs_10_) | copy-start | bytes 1241092
  43.0 33.3 %collective-permute-start.2 = (bf16[1616,128]{1,0:T(8,128)(2,1)S(1)}, bf16[1616,128]{1,0:T(8,128)(2,1)S(1)}, u32[]{:S(2)}, u32[]{:S(2)}) collective-permute-start(bf16[1616,128]{1,0:T(8,128)(2,1)S(1)} %collective-permute-done.1.refs_3_.refs_2_), channel_id=1, source_target_pairs={{0,8},{8,0},{16,24},{24,16},{32,40},{40,32},{48,56},{56,48},{64,72... | collective-permute-start | bytes 1241096 | tf_op jit(solution)/shard_map/ppermute | solution.py:419
  50.6 25.8 %collective-permute-start.4 = (bf16[1616,128]{1,0:T(8,128)(2,1)S(1)}, bf16[1616,128]{1,0:T(8,128)(2,1)}, u32[]{:S(2)}, u32[]{:S(2)}) collective-permute-start(bf16[1616,128]{1,0:T(8,128)(2,1)S(1)} %collective-permute-done.3.refs_5_.refs_4_), channel_id=1, source_target_pairs={{0,8},{8,0},{16,24},{24,16},{32,40},{40,32},{48,56},{56,48},{64,72... | collective-permute-start | bytes 1241096 | tf_op jit(solution)/shard_map/ppermute | solution.py:419
  60.5 16.3 %collective-permute-start.6 = (bf16[1616,128]{1,0:T(8,128)(2,1)S(1)}, bf16[1616,128]{1,0:T(8,128)(2,1)}, u32[]{:S(2)}, u32[]{:S(2)}) collective-permute-start(bf16[1616,128]{1,0:T(8,128)(2,1)S(1)} %collective-permute-done.5.refs_7_.refs_6_), channel_id=1, source_target_pairs={{0,8},{8,0},{16,24},{24,16},{32,40},{40,32},{48,56},{56,48},{64,72... | collective-permute-start | bytes 1241096 | tf_op jit(solution)/shard_map/ppermute | solution.py:419
  75.7 36.6 %collective-permute-start.10 = (bf16[1616,128]{1,0:T(8,128)(2,1)S(1)}, bf16[1616,128]{1,0:T(8,128)(2,1)}, u32[]{:S(2)}, u32[]{:S(2)}) collective-permute-start(bf16[1616,128]{1,0:T(8,128)(2,1)S(1)} %collective-permute-done.9.refs_5_.refs_10_), channel_id=1, source_target_pairs={{0,8},{8,0},{16,24},{24,16},{32,40},{40,32},{48,56},{56,48},{64,72... | collective-permute-start | bytes 1241096 | tf_op jit(solution)/shard_map/ppermute | solution.py:419
  76.3 0.8 copy-start.13
  76.3 36.3 %collective-permute-start.12 = (bf16[1616,128]{1,0:T(8,128)(2,1)}, bf16[1616,128]{1,0:T(8,128)(2,1)}, u32[]{:S(2)}, u32[]{:S(2)}) collective-permute-start(bf16[1616,128]{1,0:T(8,128)(2,1)} %collective-permute-done.11.refs_7_.refs_12_), channel_id=1, source_target_pairs={{0,8},{8,0},{16,24},{24,16},{32,40},{40,32},{48,56},{56,48},{64,72... | collective-permute-start | bytes 1241096 | tf_op jit(solution)/shard_map/ppermute | solution.py:419
  76.4 38.1 %collective-permute-start.14 = (bf16[1616,128]{1,0:T(8,128)(2,1)}, bf16[1616,128]{1,0:T(8,128)(2,1)S(1)}, u32[]{:S(2)}, u32[]{:S(2)}) collective-permute-start(bf16[1616,128]{1,0:T(8,128)(2,1)} %collective-permute-done.13.refs_9_.refs_14_), channel_id=1, source_target_pairs={{0,8},{8,0},{16,24},{24,16},{32,40},{40,32},{48,56},{56,48},{64,72... | collective-permute-start | bytes 1241096 | tf_op jit(solution)/shard_map/ppermute | solution.py:419
  76.8 39.0 %collective-permute-start.8 = (bf16[1616,128]{1,0:T(8,128)(2,1)}, bf16[1616,128]{1,0:T(8,128)(2,1)S(1)}, u32[]{:S(2)}, u32[]{:S(2)}) collective-permute-start(bf16[1616,128]{1,0:T(8,128)(2,1)} %collective-permute-done.7.refs_3_.refs_8_), channel_id=1, source_target_pairs={{0,8},{8,0},{16,24},{24,16},{32,40},{40,32},{48,56},{56,48},{64,72... | collective-permute-start | bytes 1241096 | tf_op jit(solution)/shard_map/ppermute | solution.py:419
  77.1 35.2 %copy-start.1 = (bf16[2,512,1024]{2,1,0:T(8,128)(2,1)S(1)}, bf16[2,512,1024]{2,1,0:T(8,128)(2,1)}, u32[]{:S(2)}) copy-start(bf16[2,512,1024]{2,1,0:T(8,128)(2,1)} %wo_own.1) | copy-start | bytes 6291460
  112.3 101.2 %collective-permute-start.20 = (bf16[2,512,1024]{2,1,0:T(8,128)(2,1)S(1)}, bf16[2,512,1024]{2,1,0:T(8,128)(2,1)}, u32[]{:S(2)}, u32[]{:S(2)}) collective-permute-start(bf16[2,512,1024]{2,1,0:T(8,128)(2,1)S(1)} %copy-done.1), channel_id=1, source_target_pairs={{0,8},{8,0},{16,24},{24,16},{32,40},{40,32},{48,56},{56,48},{64,72... | collective-permute-start | bytes 6291464 | tf_op jit(solution)/shard_map/ppermute | solution.py:418
  112.6 61.2 %collective-permute-start.16 = (bf16[2,128,1024]{2,1,0:T(8,128)(2,1)}, bf16[2,128,1024]{2,1,0:T(8,128)(2,1)S(1)}, u32[]{:S(2)}, u32[]{:S(2)}) collective-permute-start(bf16[2,128,1024]{2,1,0:T(8,128)(2,1)} %constant_dynamic-update-slice_fusion), channel_id=1, source_target_pairs={{0,1},{1,2},{2,3},{3,0},{4,5},{5,6},{6,7},{7,4},{8,9},{9,10},{10,1... | collective-permute-start | bytes 1572872 | tf_op jit(solution)/shard_map/ppermute | solution.py:422
  114.5 4.0 %copy-start.14 = (bf16[1616,128]{1,0:T(8,128)(2,1)}, bf16[1616,128]{1,0:T(8,128)(2,1)S(1)}, u32[]{:S(2)}) copy-start(bf16[1616,128]{1,0:T(8,128)(2,1)S(1)} %collective-permute-done.14.refs_10_.refs_15_) | copy-start | bytes 1241092
  114.5 59.3 %collective-permute-start.17 = (bf16[2,128,1024]{2,1,0:T(8,128)(2,1)}, bf16[2,128,1024]{2,1,0:T(8,128)(2,1)}, u32[]{:S(2)}, u32[]{:S(2)}) collective-permute-start(bf16[2,128,1024]{2,1,0:T(8,128)(2,1)} %constant_dynamic-update-slice_fusion), channel_id=1, source_target_pairs={{0,3},{1,0},{2,1},{3,2},{4,7},{5,4},{6,5},{7,6},{8,11},{9,8},{10,9... | collective-permute-start | bytes 1572872 | tf_op jit(solution)/shard_map/ppermute | solution.py:422
  115.9 2.7 %copy-start.15 = (bf16[1616,128]{1,0:T(8,128)(2,1)}, bf16[1616,128]{1,0:T(8,128)(2,1)S(1)}, u32[]{:S(2)}) copy-start(bf16[1616,128]{1,0:T(8,128)(2,1)S(1)} %collective-permute-done.8.refs_4_.refs_9_) | copy-start | bytes 1241092
  115.9 58.0 %collective-permute-start.18 = (bf16[2,128,1024]{2,1,0:T(8,128)(2,1)}, bf16[2,128,1024]{2,1,0:T(8,128)(2,1)}, u32[]{:S(2)}, u32[]{:S(2)}) collective-permute-start(bf16[2,128,1024]{2,1,0:T(8,128)(2,1)} %constant_dynamic-update-slice_fusion), channel_id=1, source_target_pairs={{0,2},{1,3},{2,0},{3,1},{4,6},{5,7},{6,4},{7,5},{8,10},{9,11},{10,... | collective-permute-start | bytes 1572872 | tf_op jit(solution)/shard_map/ppermute | solution.py:422
  169.5 10.5 %all-to-all-start = ((bf16[8,64,128]{2,1,0:T(8,128)(2,1)}), bf16[8,64,128]{2,1,0:T(8,128)(2,1)S(1)}, u32[]{:S(2)}, u32[]{:S(2)}) async-start(bf16[8,64,128]{2,1,0:T(8,128)(2,1)} %bitcast.53), calls=%async_computation | async-start | bytes 262144 | tf_op jit(solution)/shard_map/all_to_all | solution.py:434
  173.8 6.2 %copy-start.5 = (bf16[2,128,1024]{2,1,0:T(8,128)(2,1)}, bf16[2,128,1024]{2,1,0:T(8,128)(2,1)S(1)}, u32[]{:S(2)}) copy-start(bf16[2,128,1024]{2,1,0:T(8,128)(2,1)S(1)} %collective-permute-done.16.w2) | copy-start | bytes 1572868
  180.0 0.7 copy-start.4
  186.2 27.3 %all-to-all-start.1 = ((bf16[8,64,1024]{2,1,0:T(8,128)(2,1)}), bf16[8,64,1024]{2,1,0:T(8,128)(2,1)S(1)}, u32[]{:S(2)}, u32[]{:S(2)}) async-start(bf16[8,64,1024]{2,1,0:T(8,128)(2,1)} %broadcast_in_dim.46), calls=%async_computation.1 | async-start | bytes 2097152 | tf_op jit(solution)/shard_map/all_to_all | solution.py:441
  213.5 1.0 copy-start
  227.2 20.2 %copy-start.6 = (f32[64,1024]{1,0:T(8,128)S(1)}, f32[64,1024]{1,0:T(8,128)}, u32[]{:S(2)}) copy-start(f32[64,1024]{1,0:T(8,128)} %get-tuple-element.21) | copy-start | bytes 786436

commit v2 on v1

v2 whole, which is shorter than its diff:
```python
import functools

import jax
import jax.numpy as jnp
from jax import lax
from jax.experimental import pallas as pl
from jax.experimental.pallas import tpu as pltpu
from jax.sharding import PartitionSpec as P

SCALE = 0.015625
EPS = 1e-06
HD = 64
NV = 80
TD = 512
PRE = 1024
ROWS = 64
TQ = 512
NQ = 2 * TD
GATE_AT = PRE + TD
SEG_AT = GATE_AT + ROWS
PAY = SEG_AT + 16
LIMIT = 1e26
NEG = -1e30
NT = (((1,), (1,)), ((), ()))
F32 = jnp.float32
BF = jnp.bfloat16


def seq_perm(move):
    return [
        (x * 8 + y * 2 + c, (lambda t: t[0] * 8 + t[1] * 2 + t[2])(move(x, y, c)))
        for x in range(2)
        for y in range(4)
        for c in range(2)
    ]


def tp_perm(move):
    return [(q * 4 + z, (lambda t: t[0] * 4 + t[1])(move(q, z))) for q in range(2) for z in range(4)]


CORE = seq_perm(lambda x, y, c: (x, y, 1 - c))
SHIFTS = [((0, 1), (0, 3)), ((1, 0), (0, 2)), ((1, 1), (1, 3)), ((1, 2), (1, 2))]
CHIP_GROUPS = [[x * 8 + y * 2 + c for x in range(2) for y in range(4)] for c in range(2)]


def rms(wide, gain):
    mean_square = jnp.mean(wide * wide, axis=-1, keepdims=True)
    return wide * lax.rsqrt(mean_square + EPS) * gain


def project_kernel(
    tok_ref, gain_ref, w_ref, pre_ref, seg_ref, route_ref, weight_ref, pay_ref, q_ref, new_ref
):
    normed = rms(tok_ref[...].astype(F32), gain_ref[...]).astype(BF)
    proj = jnp.dot(normed, w_ref[...], preferred_element_type=F32)
    pq = proj[:, :128].astype(BF).astype(F32) * SCALE
    low = lax.broadcasted_iota(jnp.int32, (TD, 128), 1) < HD
    q_ref[:TD, :] = jnp.where(low, pq, 0.0).astype(BF)
    q_ref[TD:, :] = jnp.where(low, pltpu.roll(pq, HD, 1), 0.0).astype(BF)
    new = proj[:, 128:].astype(BF)
    new_ref[...] = new
    pay_ref[:PRE, :] = pre_ref[...]
    pay_ref[PRE:GATE_AT, :] = new
    lane = lax.broadcasted_iota(jnp.int32, (ROWS, 128), 1)
    table = jnp.zeros((ROWS, 128), F32)
    for k in range(8):
        expert = route_ref[:, k : k + 1]
        weight = weight_ref[:, k : k + 1]
        high = weight.astype(BF).astype(F32)
        table = table + jnp.where(lane == expert, high, 0.0)
        table = table + jnp.where(lane == expert + 32, weight - high, 0.0)
    pay_ref[GATE_AT:SEG_AT, :] = table.astype(BF)
    segs = jnp.concatenate([seg_ref[...].astype(F32), jnp.full((12, 128), -1.0, F32)], axis=0)
    pay_ref[SEG_AT:, :] = segs.astype(BF)


def values_t(kv):
    row = lax.broadcasted_iota(jnp.int32, (NV, 128), 0)
    col = lax.broadcasted_iota(jnp.int32, (NV, 128), 1)
    pick = jnp.where((col == row + HD) & (row < HD), 1.0, 0.0).astype(BF)
    vt = lax.dot_general(pick, kv, NT, preferred_element_type=F32)
    ones = lax.broadcasted_iota(jnp.int32, vt.shape, 0) >= HD
    return jnp.where(ones, 1.0, vt).astype(BF)


def online_step(q, kv, o_ref, m_ref, cols, mask):
    s = lax.dot_general(kv, q, NT, preferred_element_type=F32)
    if mask is not None:
        s = jnp.where(mask, s, NEG)
    m0 = m_ref[0:1, cols]
    m1 = jnp.maximum(m0, jnp.max(s, axis=0, keepdims=True))
    p = jnp.exp(s - m1).astype(BF)
    o_ref[:, cols] = o_ref[:, cols] * jnp.exp(m0 - m1) + jnp.dot(
        values_t(kv), p, preferred_element_type=F32
    )
    m_ref[0:1, cols] = m1


def pieces(ref, which, rows):
    if len(ref.shape) == 2:
        return [ref.at[rows, :]]
    return [ref.at[i, rows, :] for i in which]


def prefix_kernel(*refs, shapes, first):
    q_ref = refs[0]
    at = 1
    if not first:
        o_in, m_in = refs[1:3]
        at = 3
    pays = refs[at : at + len(shapes)]
    o_ref, m_ref, buf, sem = refs[at + len(shapes) :]
    parts = [v for p in pays for v in pieces(p, (0, 1), pl.ds(0, PRE))]
    count = len(parts)
    for j in range(count):
        pltpu.make_async_copy(parts[j], buf.at[j], sem.at[j]).start()

    def wait(j):
        pltpu.make_async_copy(parts[0], buf.at[j], sem.at[j]).wait()

    def begin():
        if first:
            o_ref[...] = jnp.zeros_like(o_ref)
        else:
            o_ref[...] = o_in[...]
            m_ref[...] = m_in[...]

    begin()
    if first:
        wait(0)
        s = lax.dot_general(buf[0, :256, :], q_ref[...], NT, preferred_element_type=F32)
        m_ref[...] = jnp.broadcast_to(jnp.max(s, axis=0, keepdims=True), m_ref.shape)

    def block(j, _):
        if first:
            pl.when(j > 0)(lambda: wait(j))
        else:
            wait(j)
        kv = buf[j]
        vt = values_t(kv)
        for t in range(NQ // TQ):
            cols = pl.ds(t * TQ, TQ)
            s = lax.dot_general(kv, q_ref[cols, :], NT, preferred_element_type=F32)
            p = jnp.exp(s - m_ref[0:1, cols]).astype(BF)
            o_ref[:, cols] = o_ref[:, cols] + jnp.dot(vt, p, preferred_element_type=F32)
        return 0

    lax.fori_loop(0, count, block, 0)

    @pl.when(jnp.logical_not(jnp.max(o_ref[HD : HD + 1, :]) < LIMIT))
    def _():
        begin()
        if first:
            m_ref[...] = jnp.full_like(m_ref, NEG)

        def again(i, _):
            kv = buf[i // 4, pl.ds(pl.multiple_of(i % 4 * 256, 256), 256), :]
            for t in range(NQ // 256):
                cols = pl.ds(t * 256, 256)
                online_step(q_ref[cols, :], kv, o_ref, m_ref, cols, None)
            return 0

        lax.fori_loop(0, count * 4, again, 0)


def prefix_call(q, state, pays):
    shapes = [p.shape for p in pays]
    count = sum(1 if len(v) == 2 else 2 for v in shapes)
    first = state is None
    vm = pl.BlockSpec(memory_space=pltpu.VMEM)
    hbm = pl.BlockSpec(memory_space=pl.ANY)
    args = (q,) + (() if first else tuple(state)) + tuple(pays)
    return pl.pallas_call(
        functools.partial(prefix_kernel, shapes=shapes, first=first),
        in_specs=[vm] * (1 if first else 3) + [hbm] * len(shapes),
        out_specs=[vm, vm],
        out_shape=[jax.ShapeDtypeStruct((NV, NQ), F32), jax.ShapeDtypeStruct((8, NQ), F32)],
        scratch_shapes=[pltpu.VMEM((count, PRE, 128), BF), pltpu.SemaphoreType.DMA((count,))],
        cost_estimate=pl.CostEstimate(
            flops=count * PRE * NQ * 2 * 600,
            bytes_accessed=count * PRE * 256 + NQ * 256 + NV * NQ * 8,
            transcendentals=count * PRE * NQ,
        ),
        name="prefix_attention",
    )(*args)


def place():
    seq = lax.axis_index("seq")
    return seq // 8, lax.rem(seq // 2, 4), lax.rem(seq, 2)


def behind(x, y, c, k):
    a, b = SHIFTS[k]
    i = jnp.where(c == 0, a[0], b[0])
    j = jnp.where(c == 0, a[1], b[1])
    return lax.rem(x - i + 2, 2), lax.rem(y - j + 4, 4)


def sources():
    x, y, c = place()
    d = 1 - c
    out = [x * 8 + y * 2 + c, x * 8 + y * 2 + d]
    for k in range(4):
        a, b = behind(x, y, c, k)
        e, f = behind(x, y, d, k)
        far, near = a * 8 + b * 2, e * 8 + f * 2
        out += [far + c, far + d, near + d, near + c] if k < 3 else [far + c, near + d]
    return out


def suffix_kernel(q_ref, o_in, m_in, qseg_ref, start_ref, *refs):
    out_ref, o_ref, m_ref, buf, segs, sem = refs[10:]
    src = sources()
    own = src[0]
    news = [v for p in refs[:10] for v in pieces(p, (0, 1), pl.ds(PRE, TD))]
    marks = [v for p in refs[:10] for v in pieces(p, (0, 1), pl.ds(SEG_AT, 16))]
    copies = []
    for j in range(16):
        at = pl.multiple_of(src[j] * TD, TD)
        copies.append(pltpu.make_async_copy(marks[j], segs.at[j], sem.at[1, j]))
        copies.append(pltpu.make_async_copy(news[j], buf.at[pl.ds(at, TD), :], sem.at[0, j]))
    for v in copies:
        v.start()
    for v in copies[::2]:
        v.wait()
    mine = jnp.max(jnp.where(lax.broadcasted_iota(jnp.int32, (1, NQ), 1) == 0, qseg_ref[...], -1.0))
    count = jnp.zeros((16, 128), F32)
    for j in range(16):
        same = (segs[j].astype(F32) == mine) & (src[j] < own)
        count = count + jnp.where(same, 1.0, 0.0)
    back = jnp.sum(count).astype(jnp.int32)
    begin_at = own * TD - back
    start = jnp.where(qseg_ref[...] == mine, begin_at, start_ref[...] + own * TD)
    for v in copies[1::2]:
        v.wait()
    lane = lax.broadcasted_iota(jnp.int32, (1, NQ), 1)
    last = own * TD + jnp.where(lane >= TD, lane - TD, lane)
    o_ref[...] = o_in[...]
    m_ref[...] = m_in[...]
    low = begin_at // TD
    latest = jnp.max(start)

    def mask_of(at, size, cols, width):
        key = at + lax.broadcasted_iota(jnp.int32, (size, width), 0)
        return (key >= cols[0]) & (key <= cols[1])

    def block(b, masked):
        at = pl.multiple_of(b * TD, TD)
        kv = buf[pl.ds(at, TD), :]
        vt = values_t(kv)
        for t in range(2):
            cols = pl.ds(t * TD, TD)
            s = lax.dot_general(kv, q_ref[cols, :], NT, preferred_element_type=F32)
            if masked:
                span = (start[:, t * TD : t * TD + TD], last[:, t * TD : t * TD + TD])
                s = jnp.where(mask_of(at, TD, span, TD), s, NEG)
            p = jnp.exp(s - m_ref[0:1, cols]).astype(BF)
            o_ref[:, cols] = o_ref[:, cols] + jnp.dot(vt, p, preferred_element_type=F32)

    def step(b, _):
        whole = (latest <= b * TD) & (b < own)
        pl.when(whole)(lambda: block(b, False))
        pl.when(jnp.logical_not(whole))(lambda: block(b, True))
        return 0

    lax.fori_loop(low, own + 1, step, 0)

    @pl.when(jnp.logical_not(jnp.max(o_ref[HD : HD + 1, :]) < LIMIT))
    def _():
        o_ref[...] = o_in[...]
        m_ref[...] = m_in[...]

        def again(i, _):
            at = pl.multiple_of(i * 256, 256)
            kv = buf[pl.ds(at, 256), :]
            for t in range(4):
                cols = pl.ds(t * 256, 256)
                span = (start[:, t * 256 : t * 256 + 256], last[:, t * 256 : t * 256 + 256])
                online_step(q_ref[cols, :], kv, o_ref, m_ref, cols, mask_of(at, 256, span, 256))
            return 0

        lax.fori_loop(low * 2, own * 2 + 2, again, 0)

    total = o_ref[...]
    mixed = total[:HD, :] / total[HD : HD + 1, :]
    both = jnp.concatenate([mixed[:, :TD], mixed[:, TD:]], axis=0)
    out_ref[...] = jnp.transpose(both).astype(BF)


def suffix_call(q, state, qseg, start, pays):
    vm = pl.BlockSpec(memory_space=pltpu.VMEM)
    hbm = pl.BlockSpec(memory_space=pl.ANY)
    return pl.pallas_call(
        suffix_kernel,
        in_specs=[vm] * 5 + [hbm] * 10,
        out_specs=vm,
        out_shape=jax.ShapeDtypeStruct((TD, 128), BF),
        scratch_shapes=[
            pltpu.VMEM((NV, NQ), F32),
            pltpu.VMEM((8, NQ), F32),
            pltpu.VMEM((16 * TD, 128), BF),
            pltpu.VMEM((16, 16, 128), BF),
            pltpu.SemaphoreType.DMA((2, 16)),
        ],
        cost_estimate=pl.CostEstimate(
            flops=6 * TD * NQ * 2 * 600, bytes_accessed=16 * TD * 256, transcendentals=6 * TD * NQ
        ),
        name="suffix_attention",
    )(q, state[0], state[1], qseg, start, *pays)


def mix_kernel(att_ref, tok_hbm, gain_ref, w0, w1, w2, w3, w4, res_ref, xi_ref, tok, sem):
    tp = lax.axis_index("tp")
    fetch = pltpu.make_async_copy(
        tok_hbm.at[pl.ds(pl.multiple_of(tp * ROWS, ROWS), ROWS), :], tok, sem
    )
    fetch.start()
    q, z = tp // 4, lax.rem(tp, 4)
    parts = [w0.at[0], w1.at[0]] + [w.at[i] for w in (w2, w3, w4) for i in range(2)]
    total = jnp.zeros((ROWS, 1024), F32)
    for j in range(8):
        head = (q if j % 2 == 0 else 1 - q) * 4 + lax.rem(z - (0, 1, 3, 2)[j // 2] + 4, 4)
        total = total + jnp.dot(att_ref[head], parts[j][...], preferred_element_type=F32)
    fetch.wait()
    total = tok[...].astype(F32) + total
    res_ref[...] = total
    xi = rms(total, gain_ref[...]).astype(BF)
    for j in range(8):
        xi_ref[j] = xi


def mix_call(att, tokens, gain, ws):
    vm = pl.BlockSpec(memory_space=pltpu.VMEM)
    return pl.pallas_call(
        mix_kernel,
        in_specs=[vm, pl.BlockSpec(memory_space=pl.ANY), vm] + [vm] * 5,
        out_specs=[vm, vm],
        out_shape=[
            jax.ShapeDtypeStruct((ROWS, 1024), F32),
            jax.ShapeDtypeStruct((8, ROWS, 1024), BF),
        ],
        scratch_shapes=[pltpu.VMEM((ROWS, 1024), BF), pltpu.SemaphoreType.DMA],
        name="mix",
    )(att, tokens, gain, *ws)


def expert_kernel(x_ref, wi_own, wi_peer, wo_own, wo_peer, *refs):
    gates = refs[:8]
    out_ref, acc, table = refs[8:]
    e = pl.program_id(0)
    x, y, c = place()

    @pl.when(e == 0)
    def _():
        chips = [(x, y)]
        for k in range(4):
            chips += [behind(x, y, c, k), behind(x, y, 1 - c, k)]
        for j in range(8):
            at = pl.multiple_of((chips[j][0] * 4 + chips[j][1]) * ROWS, ROWS)
            part = gates[j][...] if len(gates[j].shape) == 2 else gates[j][0]
            table[pl.ds(at, ROWS), :] = part.astype(F32)

    def run(wi, wo, add):
        joined = jnp.dot(x_ref[...], wi[0], preferred_element_type=F32)
        g = joined[:, :512]
        hidden = (g / (1.0 + jnp.exp(-g)) * joined[:, 512:]).astype(BF)
        o = jnp.dot(hidden, wo[0], preferred_element_type=F32).astype(BF).astype(F32)
        lane = lax.broadcasted_iota(jnp.int32, (512, 128), 1)
        side = jnp.where(e < 2, c, 1 - c)
        number = (x * 8 + y * 2 + side) * 2 + lax.rem(e, 2)
        hit = (lane == number) | (lane == number + 32)
        gate = jnp.sum(jnp.where(hit, table[...], 0.0), axis=1, keepdims=True)
        o = o * gate
        if add:
            acc[...] = acc[...] + o
        else:
            acc[...] = o

    pl.when(e == 0)(lambda: run(wi_own, wo_own, False))
    pl.when(e == 1)(lambda: run(wi_own, wo_own, True))
    pl.when(e >= 2)(lambda: run(wi_peer, wo_peer, True))

    @pl.when(e == 3)
    def _():
        out_ref[...] = acc[...].astype(BF)


def expert_call(x, wi_own, wi_peer, wo_own, wo_peer, pays):
    own = lambda e: (jnp.minimum(e, 1), 0, 0)
    peer = lambda e: (jnp.maximum(e - 2, 0), 0, 0)
    flat = pl.BlockSpec((ROWS, 128), lambda e: (GATE_AT // ROWS, 0))

    def pair(i):
        return pl.BlockSpec((1, ROWS, 128), lambda e: (i, GATE_AT // ROWS, 0))

    return pl.pallas_call(
        expert_kernel,
        grid=(4,),
        in_specs=[
            pl.BlockSpec((512, 1024), lambda e: (0, 0)),
            pl.BlockSpec((1, 1024, 1024), own),
            pl.BlockSpec((1, 1024, 1024), peer),
            pl.BlockSpec((1, 512, 1024), own),
            pl.BlockSpec((1, 512, 1024), peer),
            flat,
        ]
        + [pair(i) for _ in range(3) for i in range(2)]
        + [flat],
        out_specs=pl.BlockSpec((512, 1024), lambda e: (0, 0)),
        scratch_shapes=[pltpu.VMEM((512, 1024), F32), pltpu.VMEM((512, 128), F32)],
        out_shape=jax.ShapeDtypeStruct((512, 1024), BF),
        name="experts",
    )(x, wi_own, wi_peer, wo_own, wo_peer, *pays)


def body(
    tokens,
    segment_ids,
    prefix_cache,
    norm1_gain,
    w_qkv,
    w_out,
    norm2_gain,
    expert_in,
    expert_out,
    routes,
    route_weights,
):
    pay, q, new = pl.pallas_call(
        project_kernel,
        out_shape=[
            jax.ShapeDtypeStruct((PAY, 128), BF),
            jax.ShapeDtypeStruct((NQ, 128), BF),
            jax.ShapeDtypeStruct((TD, 128), BF),
        ],
        name="project",
    )(
        tokens,
        norm1_gain[None, :],
        w_qkv.reshape(1024, 256),
        prefix_cache.reshape(PRE, 128),
        segment_ids.reshape(4, 128),
        routes,
        route_weights,
    )
    tie = lax.optimization_barrier

    wx = lax.ppermute(w_out, "tp", tp_perm(lambda a, b: (1 - a, b)))
    near0 = lax.ppermute(pay, "seq", CORE)
    state = prefix_call(q, None, [pay])
    near0, wx, state = tie((near0, wx, state))
    pair = jnp.stack([pay, near0])

    def ahead(k):
        return seq_perm(
            lambda a, b, d: ((a + SHIFTS[k][d][0]) % 2, (b + SHIFTS[k][d][1]) % 4, d)
        )

    far = [lax.ppermute(pair, "seq", ahead(k)) for k in range(3)]
    far.append(lax.ppermute(pay, "seq", ahead(3)))
    segment_ids, state = tie((segment_ids, state))
    segf = segment_ids.astype(F32)
    local = jnp.sum((segment_ids[:, None] < segment_ids[None, :]).astype(jnp.int32), axis=0)
    start = jnp.concatenate([local, local])[None, :]
    qseg = jnp.concatenate([segf, segf])[None, :]
    state = prefix_call(q, state, [near0])

    far[0], far[1], state = tie((far[0], far[1], state))
    near = [lax.ppermute(far[k], "seq", CORE) for k in range(2)]
    wpair = jnp.concatenate([w_out, wx])
    wz = [lax.ppermute(wpair, "tp", tp_perm(lambda a, b, k=k: (a, (b + k) % 4))) for k in (1, 3, 2)]
    state = prefix_call(q, state, [far[0], far[1]])
    near[0], near[1], far[2], far[3], state = tie((near[0], near[1], far[2], far[3], state))
    near += [lax.ppermute(far[k], "seq", CORE) for k in range(2, 4)]
    state = prefix_call(q, state, [near[0], near[1], far[2], far[3]])
    expert_in, expert_out, state = tie((expert_in, expert_out, state))
    wi_peer = lax.ppermute(expert_in, "seq", CORE)
    wo_peer = lax.ppermute(expert_out, "seq", CORE)
    state = prefix_call(q, state, [near[2], near[3]])
    pays = [pay, near0] + [v for k in range(4) for v in (far[k], near[k])]
    attended = suffix_call(q, state, qseg, start, pays)

    spread = lax.all_to_all(attended.reshape(8, ROWS, 128), "tp", 0, 0, tiled=True)
    residual, copies = mix_call(spread, tokens, norm2_gain[None, :], [w_out, wx] + wz)
    everyone = lax.all_to_all(copies, "seq", 0, 0, axis_index_groups=CHIP_GROUPS, tiled=True)
    partial = expert_call(
        everyone.reshape(512, 1024),
        expert_in,
        wi_peer,
        expert_out,
        wo_peer,
        [pay, far[0], near[0], far[1], near[1], far[2], near[2], far[3]],
    )
    returned = lax.all_to_all(
        partial.reshape(8, ROWS, 1024), "seq", 0, 0, axis_index_groups=CHIP_GROUPS, tiled=True
    )
    hidden = (residual + jnp.sum(returned.astype(F32), axis=0)).astype(BF)
    return hidden, new.reshape(TD, 1, 128)


def solution(mesh):
    in_specs = (
        P("seq", None),
        P("seq"),
        P("seq", "tp", None),
        P(),
        P(None, "tp", None),
        P("tp", None, None),
        P(),
        P("seq", None, None),
        P("seq", None, None),
        P(("seq", "tp"), None),
        P(("seq", "tp"), None),
    )
    out_specs = (P(("seq", "tp"), None), P("seq", "tp", None))
    return jax.shard_map(body, mesh=mesh, in_specs=in_specs, out_specs=out_specs, check_vma=False)
```

time: 250 us -> 230 us (0.920)
  blocking collectives: 20 us -> 42.6 us
  waiting for transfers between devices: 43.1 us -> 21.2 us
  local copies, waits for them, and re-layouts: 18.5 us -> 5.63 us
  starting transfers between devices: 42.1 us -> 35.6 us
    all_to_all x0 -> x1, blocking collectives: none -> 26 us  [body(): lax.all_to_all(copies, 'seq', 0, 0, axis_index_groups=CHIP_GROUPS, tiled=...]
    ppermute x15 -> x9, waiting for transfers between devices: 28.3 us -> 11.3 us  [the longest x3 7.89 us: body(): far = [lax.ppermute(pair, 'seq', ahead(k)) for k in range(3)]]
    all_to_all x1 -> x0, starting transfers between devices: 14.6 us -> none  [body(): lax.all_to_all(jnp.broadcast_to(xi[None], (8, ROWS, 1024)), 'seq', 0, 0,...]
    slice x8 -> x0, local copies, waits for them, and re-layouts: 10.5 us -> none  [body(): gate_parts = [p[GATE_AT:] for p in [pay] + far]]
    ppermute x15 -> x9, starting transfers between devices: 16 us -> 20 us  [the longest x2 8.04 us: body(): near = [lax.ppermute(far[k], 'seq', CORE) for k in range(2)]]
    ppermute x1, waiting for transfers between devices: 7.15 us -> 3.19 us  [body(): wx = lax.ppermute(w_out, 'tp', tp_perm(lambda a, b: (1 - a, b)))]
    all_to_all x1, blocking collectives: 20 us -> 16.5 us  [body(): lax.all_to_all(partial.reshape(8, ROWS, 1024), 'seq', 0, 0, axis_index_gr...]
    ppermute x3, starting transfers between devices: 5.9 us -> 8.86 us  [body(): lax.ppermute(wpair, 'tp', tp_perm(lambda a, b, k=k: (a, (b + k) % 4)))]
  transfers between devices with their start and end apart: 23 -> 16, of which waited for: 7 -> 5; matrix products, arithmetic and copies ran while one was open for 7% -> 1% of each run, Pallas kernels for 42% -> 28%
where the time goes in v2:
time: 230 us; the launch traced here: 227 us
  Pallas kernels  119 us (52%)
  blocking collectives  42.6 us (19%)
  starting transfers between devices  35.6 us (15%)
  waiting for transfers between devices  21.2 us (9%)
  local copies, waits for them, and re-layouts  5.63 us (2%)
  other arithmetic  2.32 us (1%)
    pallas_call x5, Pallas kernels, prefix_call(): pl.pallas_call(functools.partial(prefix_kernel, shapes=shapes, first=firs...  94.2 us
    all_to_all x1, blocking collectives, body(): lax.all_to_all(copies, 'seq', 0, 0, axis_index_groups=CHIP_GROUPS, tiled=...  26 us
    all_to_all x1, blocking collectives, body(): lax.all_to_all(partial.reshape(8, ROWS, 1024), 'seq', 0, 0, axis_index_gr...  16.5 us
    pallas_call x1, Pallas kernels, expert_call(): pl.pallas_call(expert_kernel, grid=(4,), in_specs=[pl.BlockSpec((512, 102...  12.2 us
    ppermute x3, starting transfers between devices, body(): lax.ppermute(wpair, 'tp', tp_perm(lambda a, b, k=k: (a, (b + k) % 4)))  8.86 us
    ppermute x2, starting transfers between devices, body(): near = [lax.ppermute(far[k], 'seq', CORE) for k in range(2)]  8.04 us
    ppermute x3, waiting for transfers between devices, body(): far = [lax.ppermute(pair, 'seq', ahead(k)) for k in range(3)]  7.89 us
    ppermute x3, starting transfers between devices, body(): far = [lax.ppermute(pair, 'seq', ahead(k)) for k in range(3)]  7.1 us
  transfers between devices with their start and end apart: 16, of which 5 were waited for; matrix products, arithmetic and copies ran while one was open for 1% of the time, Pallas kernels for 28%

profile of v2, /device:TPU:0, one launch (start us, length us, event | category | flops | bytes accessed | tf_op | source)
XLA Modules:
  0.0 226.7 jit_solution(4981914461455439709)
XLA Ops:
  0.6 1.4 copy.15.route_ref
  2.0 1.4 copy.16.weight_ref
  3.4 3.1 %project.1 = (bf16[1616,128]{1,0:T(8,128)(2,1)}, bf16[1024,128]{1,0:T(8,128)(2,1)}, bf16[512,128]{1,0:T(8,128)(2,1)}) custom-call(bf16[512,1024]{1,0:T(8,128)(2,1)} %tok_hbm.1, f32[1,1024]{1,0:T(1,128)} %bitcast.21, bf16[1024,256]{1,0:T(8,128)(2,1)} %bitcast.16, bf16[1024,128]{1,0:T(8,128)(2,1)} %bitcast.18, s32[4,128]{1,0:T(4,128)} %bitcast.20, ...), custom_call_target="tpu_custom_call" | custom-call | tf_op jit(solution)/shard_map/project/pallas_call | solution.py:431
  6.5 0.0 collective-permute-start
  6.5 1.6 collective-permute-start.1
  8.1 4.2 %prefix_attention.5 = (f32[80,1024]{1,0:T(8,128)}, f32[8,1024]{1,0:T(8,128)}) custom-call(bf16[1024,128]{1,0:T(8,128)(2,1)} %get-tuple-element.38.refs_0_.q_ref, bf16[1616,128]{1,0:T(8,128)(2,1)} %get-tuple-element.39.refs_1_.refs_0_), custom_call_target="tpu_custom_call" | custom-call | flops 1258291200 | bytes 1179648 | tf_op jit(solution)/shard_map/prefix_attention/pallas_call | solution.py:174
  12.2 3.2 %collective-permute-done.1.w1 = bf16[1,128,1024]{2,1,0:T(8,128)(2,1)S(1)} collective-permute-done((bf16[1,128,1024]{2,1,0:T(8,128)(2,1)}, bf16[1,128,1024]{2,1,0:T(8,128)(2,1)S(1)}, u32[]{:S(2)}, u32[]{:S(2)}) %collective-permute-start.1) | collective-permute-done | bytes 262176 | tf_op jit(solution)/shard_map/ppermute | solution.py:450
  15.4 0.1 pad_maximum_fusion
  15.5 3.2 %collective-permute-start.3 = (bf16[2,1616,128]{2,1,0:T(8,128)(2,1)S(1)}, bf16[2,1616,128]{2,1,0:T(8,128)(2,1)S(1)}, u32[]{:S(2)}, u32[]{:S(2)}) collective-permute-start(bf16[2,1616,128]{2,1,0:T(8,128)(2,1)S(1)} %pad_maximum_fusion), channel_id=1, source_target_pairs={{0,64},{8,40},{16,80},{24,56},{32,96},{40,8},{48,112},{56,24},{64,... | collective-permute-start | bytes 2482184 | tf_op jit(solution)/shard_map/ppermute | solution.py:461
  18.7 1.6 collective-permute-start.2
  20.3 2.3 %collective-permute-start.6 = (bf16[2,1616,128]{2,1,0:T(8,128)(2,1)S(1)}, bf16[2,1616,128]{2,1,0:T(8,128)(2,1)}, u32[]{:S(2)}, u32[]{:S(2)}) collective-permute-start(bf16[2,1616,128]{2,1,0:T(8,128)(2,1)S(1)} %pad_maximum_fusion), channel_id=1, source_target_pairs={{0,80},{8,120},{16,96},{24,72},{32,112},{40,88},{48,64},{56,104},{... | collective-permute-start | bytes 2482184 | tf_op jit(solution)/shard_map/ppermute | solution.py:461
  22.6 8.1 %prefix_attention.6 = (f32[80,1024]{1,0:T(8,128)}, f32[8,1024]{1,0:T(8,128)}) custom-call(bf16[1024,128]{1,0:T(8,128)(2,1)} %get-tuple-element.38.refs_0_.q_ref, f32[80,1024]{1,0:T(8,128)} %get-tuple-element.45.refs_1_, f32[8,1024]{1,0:T(8,128)} %get-tuple-element.46.refs_2_, bf16[1616,128]{1,0:T(8,128)(2,1)} %copy-done.8), custom_call_target="tpu_custom_call" | custom-call | flops 1258291200 | bytes 1179648 | tf_op jit(solution)/shard_map/prefix_attention/pallas_call | solution.py:174
  30.8 4.4 %collective-permute-done.3.refs_4_.refs_3_ = bf16[2,1616,128]{2,1,0:T(8,128)(2,1)S(1)} collective-permute-done((bf16[2,1616,128]{2,1,0:T(8,128)(2,1)S(1)}, bf16[2,1616,128]{2,1,0:T(8,128)(2,1)S(1)}, u32[]{:S(2)}, u32[]{:S(2)}) %collective-permute-start.3) | collective-permute-done | bytes 827424 | tf_op jit(solution)/shard_map/ppermute | solution.py:461
  35.2 3.5 %collective-permute-done.2.refs_3_.refs_2_.refs_1_ = bf16[2,1616,128]{2,1,0:T(8,128)(2,1)} collective-permute-done((bf16[2,1616,128]{2,1,0:T(8,128)(2,1)S(1)}, bf16[2,1616,128]{2,1,0:T(8,128)(2,1)}, u32[]{:S(2)}, u32[]{:S(2)}) %collective-permute-start.2) | collective-permute-done | bytes 827424 | tf_op jit(solution)/shard_map/ppermute | solution.py:461
  38.6 8.0 %collective-permute-start.4 = (bf16[2,1616,128]{2,1,0:T(8,128)(2,1)}, bf16[2,1616,128]{2,1,0:T(8,128)(2,1)}, u32[]{:S(2)}, u32[]{:S(2)}) collective-permute-start(bf16[2,1616,128]{2,1,0:T(8,128)(2,1)} %collective-permute-done.2.refs_3_.refs_2_.refs_1_), channel_id=1, source_target_pairs={{0,8},{8,0},{16,24},{24,16},{32,40},{40,32},{48,56},{56,48},{64,72... | collective-permute-start | bytes 2482184 | tf_op jit(solution)/shard_map/ppermute | solution.py:471
  46.7 0.0 collective-permute-start.5
  46.7 4.4 %collective-permute-start.7 = (bf16[1616,128]{1,0:T(8,128)(2,1)S(1)}, bf16[1616,128]{1,0:T(8,128)(2,1)S(1)}, u32[]{:S(2)}, u32[]{:S(2)}) collective-permute-start(bf16[1616,128]{1,0:T(8,128)(2,1)S(1)} %copy-done.1), channel_id=1, source_target_pairs={{0,96},{8,104},{16,112},{24,120},{32,64},{40,72},{48,80},{56,88},{... | collective-permute-start | bytes 1241096 | tf_op jit(solution)/shard_map/ppermute | solution.py:462
  51.1 23.8 %prefix_attention.7 = (f32[80,1024]{1,0:T(8,128)}, f32[8,1024]{1,0:T(8,128)}) custom-call(bf16[1024,128]{1,0:T(8,128)(2,1)} %get-tuple-element.38.refs_0_.q_ref, f32[80,1024]{1,0:T(8,128)} %get-tuple-element.51.refs_1_, f32[8,1024]{1,0:T(8,128)} %get-tuple-element.52.refs_2_, bf16[2,1616,128]{2,1,0:T(8,128)(2,1)} %collective-permute-done.2.refs_3_.refs_2_.refs_1_, ...), custom_call_target="tpu_custom_call" | custom-call | flops 5033164800 | bytes 1966080 | tf_op jit(solution)/shard_map/prefix_attention/pallas_call | solution.py:174
  74.8 0.0 collective-permute-done.7.refs_6_.refs_8_.refs_7_
  74.9 0.0 collective-permute-done.6.refs_5_.refs_6_
  74.9 0.0 collective-permute-done.5.refs_4_.refs_5_
  74.9 0.7 copy-done.9
  75.6 39.6 %prefix_attention.8 = (f32[80,1024]{1,0:T(8,128)}, f32[8,1024]{1,0:T(8,128)}) custom-call(bf16[1024,128]{1,0:T(8,128)(2,1)} %get-tuple-element.38.refs_0_.q_ref, f32[80,1024]{1,0:T(8,128)} %get-tuple-element.55.refs_1_, f32[8,1024]{1,0:T(8,128)} %get-tuple-element.56.refs_2_, bf16[2,1616,128]{2,1,0:T(8,128)(2,1)} %collective-permute-done.4.refs_3_.refs_2_, ...), custom_call_target="tpu_custom_call" | custom-call | flops 8808038400 | bytes 2752512 | tf_op jit(solution)/shard_map/prefix_attention/pallas_call | solution.py:174
  115.2 0.3 collective-permute-start.13
  115.5 0.3 collective-permute-start.8
  115.8 0.7 constant_dynamic-update-slice_fusion.1
  116.5 0.2 collective-permute-start.9
  116.8 0.3 collective-permute-start.14
  117.1 0.7 constant_dynamic-update-slice_fusion
  117.8 3.8 %collective-permute-start.12 = (bf16[2,128,1024]{2,1,0:T(8,128)(2,1)}, bf16[2,128,1024]{2,1,0:T(8,128)(2,1)S(1)}, u32[]{:S(2)}, u32[]{:S(2)}) collective-permute-start(bf16[2,128,1024]{2,1,0:T(8,128)(2,1)} %constant_dynamic-update-slice_fusion), channel_id=1, source_target_pairs={{0,2},{1,3},{2,0},{3,1},{4,6},{5,7},{6,4},{7,5},{8,10},{9,11},{10,... | collective-permute-start | bytes 1572872 | tf_op jit(solution)/shard_map/ppermute | solution.py:473
  121.6 0.2 convert_reduce_fusion.1
  121.8 0.6 pad_add_fusion
  122.4 0.6 pad_maximum_fusion.1
  123.0 3.4 %collective-permute-done.9.refs_4_.refs_9_ = bf16[1616,128]{1,0:T(8,128)(2,1)} collective-permute-done((bf16[1616,128]{1,0:T(8,128)(2,1)}, bf16[1616,128]{1,0:T(8,128)(2,1)}, u32[]{:S(2)}, u32[]{:S(2)}) %collective-permute-start.9) | collective-permute-done | bytes 413728 | tf_op jit(solution)/shard_map/ppermute | solution.py:476
  126.4 5.1 %collective-permute-start.11 = (bf16[2,128,1024]{2,1,0:T(8,128)(2,1)}, bf16[2,128,1024]{2,1,0:T(8,128)(2,1)S(1)}, u32[]{:S(2)}, u32[]{:S(2)}) collective-permute-start(bf16[2,128,1024]{2,1,0:T(8,128)(2,1)} %constant_dynamic-update-slice_fusion), channel_id=1, source_target_pairs={{0,3},{1,0},{2,1},{3,2},{4,7},{5,4},{6,5},{7,6},{8,11},{9,8},{10,9... | collective-permute-start | bytes 1572872 | tf_op jit(solution)/shard_map/ppermute | solution.py:473
  131.4 0.0 collective-permute-start.10
  131.4 18.6 %prefix_attention.9 = (f32[80,1024]{1,0:T(8,128)}, f32[8,1024]{1,0:T(8,128)}) custom-call(bf16[1024,128]{1,0:T(8,128)(2,1)} %get-tuple-element.38.refs_0_.q_ref, f32[80,1024]{1,0:T(8,128)} %get-tuple-element.63.refs_1_, f32[8,1024]{1,0:T(8,128)} %get-tuple-element.64.refs_2_, bf16[2,1616,128]{2,1,0:T(8,128)(2,1)} %collective-permute-done.8.refs_3_.refs_7_.refs_6_, ...), custom_call_target="tpu_custom_call" | custom-call | flops 3774873600 | bytes 1703936 | tf_op jit(solution)/shard_map/prefix_attention/pallas_call | solution.py:174
  150.0 5.2 %suffix_attention.1 = bf16[512,128]{1,0:T(8,128)(2,1)} custom-call(bf16[1024,128]{1,0:T(8,128)(2,1)} %get-tuple-element.38.refs_0_.q_ref, f32[80,1024]{1,0:T(8,128)} %get-tuple-element.65.o_in, f32[8,1024]{1,0:T(8,128)} %get-tuple-element.66.m_in, f32[1,1024]{1,0:T(1,128)} %bitcast.24, s32[1,1024]{1,0:T(1,128)} %bitcast.23, ...), custom_call_target="tpu_custom_call" | custom-call | flops 3774873600 | bytes 2097152 | tf_op jit(solution)/shard_map/suffix_attention/pallas_call | solution.py:295
  155.2 4.5 %all-to-all-start = ((bf16[8,64,128]{2,1,0:T(8,128)(2,1)}), bf16[8,64,128]{2,1,0:T(8,128)(2,1)S(1)}, u32[]{:S(2)}, u32[]{:S(2)}) async-start(bf16[8,64,128]{2,1,0:T(8,128)(2,1)} %bitcast.19), calls=%async_computation | async-start | bytes 262144 | tf_op jit(solution)/shard_map/all_to_all | solution.py:485
  159.8 0.0 collective-permute-done.11.w3
  159.8 6.7 %all-to-all-done.att_ref = bf16[8,64,128]{2,1,0:T(8,128)(2,1)S(1)} async-done(((bf16[8,64,128]{2,1,0:T(8,128)(2,1)}), bf16[8,64,128]{2,1,0:T(8,128)(2,1)S(1)}, u32[]{:S(2)}, u32[]{:S(2)}) %all-to-all-start) | async-done | bytes 131104 | tf_op jit(solution)/shard_map/all_to_all | solution.py:485
  166.5 0.6 copy-done.7
  167.2 3.9 %mix.1 = (f32[64,1024]{1,0:T(8,128)}, bf16[8,64,1024]{2,1,0:T(8,128)(2,1)}) custom-call(bf16[8,64,128]{2,1,0:T(8,128)(2,1)} %copy-done.7, bf16[512,1024]{1,0:T(8,128)(2,1)} %tok_hbm.1, f32[1,1024]{1,0:T(1,128)} %bitcast.22, bf16[1,128,1024]{2,1,0:T(8,128)(2,1)} %w0.1, bf16[1,128,1024]{2,1,0:T(8,128)(2,1)} %copy-done.3, ...), custom_call_target="tpu_custom_call" | custom-call | tf_op jit(solution)/shard_map/mix/pallas_call | solution.py:336
  171.1 26.0 %all_to_all.15 = bf16[8,64,1024]{2,1,0:T(8,128)(2,1)} all-to-all(bf16[8,64,1024]{2,1,0:T(8,128)(2,1)} %get-tuple-element.70), channel_id=1, replica_groups={{0,16,32,48,64,80,96,112},{8,24,40,56,72,88,104,120},{1,17,33,49,65,81,..., dimensions={0} | all-to-all | bytes 2097152 | tf_op jit(solution)/shard_map/all_to_all | solution.py:487
  197.1 12.2 %experts.1 = bf16[512,1024]{1,0:T(8,128)(2,1)} custom-call(bf16[512,1024]{1,0:T(8,128)(2,1)} %bitcast.13, bf16[2,1024,1024]{2,1,0:T(8,128)(2,1)} %wi_own, bf16[2,1024,1024]{2,1,0:T(8,128)(2,1)} %collective-permute-done.13.wi_peer, bf16[2,512,1024]{2,1,0:T(8,128)(2,1)} %wo_own, bf16[2,512,1024]{2,1,0:T(8,128)(2,1)} %collective-permute-done.14.wo_peer, ...), custom_call_target="tpu_custom_call" | custom-call | tf_op jit(solution)/shard_map/experts/pallas_call | solution.py:398
  209.3 16.5 %all_to_all.16 = bf16[8,64,1024]{2,1,0:T(8,128)(2,1)S(1)} all-to-all(bf16[8,64,1024]{2,1,0:T(8,128)(2,1)} %bitcast.14), channel_id=1, replica_groups={{0,16,32,48,64,80,96,112},{8,24,40,56,72,88,104,120},{1,17,33,49,65,81,..., dimensions={0} | all-to-all | bytes 2097152 | tf_op jit(solution)/shard_map/all_to_all | solution.py:496
  225.9 0.2 convert_reduce_fusion
  226.1 0.7 add_convert_fusion
  (30 shorter events, 0.1 us)
Async XLA Ops:
  6.5 8.9 %collective-permute-start = (bf16[1616,128]{1,0:T(8,128)(2,1)}, bf16[1616,128]{1,0:T(8,128)(2,1)S(1)}, u32[]{:S(2)}, u32[]{:S(2)}) collective-permute-start(bf16[1616,128]{1,0:T(8,128)(2,1)} %get-tuple-element.39.refs_1_.refs_0_), channel_id=1, source_target_pairs={{0,8},{8,0},{16,24},{24,16},{32,40},{40,32},{48,56},{56,48},{64,72... | collective-permute-start | bytes 1241096 | tf_op jit(solution)/shard_map/ppermute | solution.py:451
  6.5 8.9 %collective-permute-start.1 = (bf16[1,128,1024]{2,1,0:T(8,128)(2,1)}, bf16[1,128,1024]{2,1,0:T(8,128)(2,1)S(1)}, u32[]{:S(2)}, u32[]{:S(2)}) collective-permute-start(bf16[1,128,1024]{2,1,0:T(8,128)(2,1)} %w0.1), channel_id=1, source_target_pairs={{0,4},{1,5},{2,6},{3,7},{4,0},{5,1},{6,2},{7,3},{8,12},{9,13},{10,... | collective-permute-start | bytes 786440 | tf_op jit(solution)/shard_map/ppermute | solution.py:450
  8.0 7.4 %copy-start.1 = (bf16[1616,128]{1,0:T(8,128)(2,1)S(1)}, bf16[1616,128]{1,0:T(8,128)(2,1)}, u32[]{:S(2)}) copy-start(bf16[1616,128]{1,0:T(8,128)(2,1)} %get-tuple-element.39.refs_1_.refs_0_) | copy-start | bytes 1241092
  15.4 101.7 %copy-start.3 = (bf16[1,128,1024]{2,1,0:T(8,128)(2,1)}, bf16[1,128,1024]{2,1,0:T(8,128)(2,1)S(1)}, u32[]{:S(2)}) copy-start(bf16[1,128,1024]{2,1,0:T(8,128)(2,1)S(1)} %collective-permute-done.1.w1) | copy-start | bytes 786436
  15.4 7.2 %copy-start.8 = (bf16[1616,128]{1,0:T(8,128)(2,1)}, bf16[1616,128]{1,0:T(8,128)(2,1)S(1)}, u32[]{:S(2)}) copy-start(bf16[1616,128]{1,0:T(8,128)(2,1)S(1)} %collective-permute-done.refs_3_.refs_1_) | copy-start | bytes 1241092
  15.5 19.7 %collective-permute-start.3 = (bf16[2,1616,128]{2,1,0:T(8,128)(2,1)S(1)}, bf16[2,1616,128]{2,1,0:T(8,128)(2,1)S(1)}, u32[]{:S(2)}, u32[]{:S(2)}) collective-permute-start(bf16[2,1616,128]{2,1,0:T(8,128)(2,1)S(1)} %pad_maximum_fusion), channel_id=1, source_target_pairs={{0,64},{8,40},{16,80},{24,56},{32,96},{40,8},{48,112},{56,24},{64,... | collective-permute-start | bytes 2482184 | tf_op jit(solution)/shard_map/ppermute | solution.py:461
  18.7 20.0 %collective-permute-start.2 = (bf16[2,1616,128]{2,1,0:T(8,128)(2,1)S(1)}, bf16[2,1616,128]{2,1,0:T(8,128)(2,1)}, u32[]{:S(2)}, u32[]{:S(2)}) collective-permute-start(bf16[2,1616,128]{2,1,0:T(8,128)(2,1)S(1)} %pad_maximum_fusion), channel_id=1, source_target_pairs={{0,16},{8,56},{16,32},{24,8},{32,48},{40,24},{48,0},{56,40},{64,80... | collective-permute-start | bytes 2482184 | tf_op jit(solution)/shard_map/ppermute | solution.py:461
  20.3 54.6 %collective-permute-start.6 = (bf16[2,1616,128]{2,1,0:T(8,128)(2,1)S(1)}, bf16[2,1616,128]{2,1,0:T(8,128)(2,1)}, u32[]{:S(2)}, u32[]{:S(2)}) collective-permute-start(bf16[2,1616,128]{2,1,0:T(8,128)(2,1)S(1)} %pad_maximum_fusion), channel_id=1, source_target_pairs={{0,80},{8,120},{16,96},{24,72},{32,112},{40,88},{48,64},{56,104},{... | collective-permute-start | bytes 2482184 | tf_op jit(solution)/shard_map/ppermute | solution.py:461
  35.2 15.9 %copy-start.4 = (bf16[2,1616,128]{2,1,0:T(8,128)(2,1)}, bf16[2,1616,128]{2,1,0:T(8,128)(2,1)S(1)}, u32[]{:S(2)}) copy-start(bf16[2,1616,128]{2,1,0:T(8,128)(2,1)S(1)} %collective-permute-done.3.refs_4_.refs_3_) | copy-start | bytes 2482180
  38.6 36.2 %collective-permute-start.4 = (bf16[2,1616,128]{2,1,0:T(8,128)(2,1)}, bf16[2,1616,128]{2,1,0:T(8,128)(2,1)}, u32[]{:S(2)}, u32[]{:S(2)}) collective-permute-start(bf16[2,1616,128]{2,1,0:T(8,128)(2,1)} %collective-permute-done.2.refs_3_.refs_2_.refs_1_), channel_id=1, source_target_pairs={{0,8},{8,0},{16,24},{24,16},{32,40},{40,32},{48,56},{56,48},{64,72... | collective-permute-start | bytes 2482184 | tf_op jit(solution)/shard_map/ppermute | solution.py:471
  46.7 28.2 %collective-permute-start.5 = (bf16[2,1616,128]{2,1,0:T(8,128)(2,1)S(1)}, bf16[2,1616,128]{2,1,0:T(8,128)(2,1)}, u32[]{:S(2)}, u32[]{:S(2)}) collective-permute-start(bf16[2,1616,128]{2,1,0:T(8,128)(2,1)S(1)} %collective-permute-done.3.refs_4_.refs_3_), channel_id=1, source_target_pairs={{0,8},{8,0},{16,24},{24,16},{32,40},{40,32},{48,56},{56,48},{64,72... | collective-permute-start | bytes 2482184 | tf_op jit(solution)/shard_map/ppermute | solution.py:471
  46.7 28.2 %collective-permute-start.7 = (bf16[1616,128]{1,0:T(8,128)(2,1)S(1)}, bf16[1616,128]{1,0:T(8,128)(2,1)S(1)}, u32[]{:S(2)}, u32[]{:S(2)}) collective-permute-start(bf16[1616,128]{1,0:T(8,128)(2,1)S(1)} %copy-done.1), channel_id=1, source_target_pairs={{0,96},{8,104},{16,112},{24,120},{32,64},{40,72},{48,80},{56,88},{... | collective-permute-start | bytes 1241096 | tf_op jit(solution)/shard_map/ppermute | solution.py:462
  74.8 0.8 copy-start.9
  75.6 40.2 %copy-start.2 = (bf16[1,128,1024]{2,1,0:T(8,128)(2,1)S(1)}, bf16[1,128,1024]{2,1,0:T(8,128)(2,1)}, u32[]{:S(2)}) copy-start(bf16[1,128,1024]{2,1,0:T(8,128)(2,1)} %w0.1) | copy-start | bytes 786436
  75.6 41.2 %copy-start = (bf16[2,512,1024]{2,1,0:T(8,128)(2,1)S(1)}, bf16[2,512,1024]{2,1,0:T(8,128)(2,1)}, u32[]{:S(2)}) copy-start(bf16[2,512,1024]{2,1,0:T(8,128)(2,1)} %wo_own) | copy-start | bytes 6291460
  75.6 42.2 %copy-start.11 = (s32[512]{0:T(512)S(1)}, s32[512]{0:T(512)}, u32[]{:S(2)}) copy-start(s32[512]{0:T(512)} %param.12) | copy-start | bytes 6148
  115.2 81.9 %collective-permute-start.13 = (bf16[2,1024,1024]{2,1,0:T(8,128)(2,1)}, bf16[2,1024,1024]{2,1,0:T(8,128)(2,1)}, u32[]{:S(2)}, u32[]{:S(2)}) collective-permute-start(bf16[2,1024,1024]{2,1,0:T(8,128)(2,1)} %wi_own), channel_id=1, source_target_pairs={{0,8},{8,0},{16,24},{24,16},{32,40},{40,32},{48,56},{56,48},{64,72... | collective-permute-start | bytes 12582920 | tf_op jit(solution)/shard_map/ppermute | solution.py:479
  115.5 15.9 %collective-permute-start.8 = (bf16[2,1616,128]{2,1,0:T(8,128)(2,1)}, bf16[2,1616,128]{2,1,0:T(8,128)(2,1)}, u32[]{:S(2)}, u32[]{:S(2)}) collective-permute-start(bf16[2,1616,128]{2,1,0:T(8,128)(2,1)} %collective-permute-done.6.refs_5_.refs_6_), channel_id=1, source_target_pairs={{0,8},{8,0},{16,24},{24,16},{32,40},{40,32},{48,56},{56,48},{64,72... | collective-permute-start | bytes 2482184 | tf_op jit(solution)/shard_map/ppermute | solution.py:476
  116.5 9.8 %collective-permute-start.9 = (bf16[1616,128]{1,0:T(8,128)(2,1)}, bf16[1616,128]{1,0:T(8,128)(2,1)}, u32[]{:S(2)}, u32[]{:S(2)}) collective-permute-start(bf16[1616,128]{1,0:T(8,128)(2,1)} %copy-done.9), channel_id=1, source_target_pairs={{0,8},{8,0},{16,24},{24,16},{32,40},{40,32},{48,56},{56,48},{64,72... | collective-permute-start | bytes 1241096 | tf_op jit(solution)/shard_map/ppermute | solution.py:476
  116.8 80.3 %collective-permute-start.14 = (bf16[2,512,1024]{2,1,0:T(8,128)(2,1)S(1)}, bf16[2,512,1024]{2,1,0:T(8,128)(2,1)}, u32[]{:S(2)}, u32[]{:S(2)}) collective-permute-start(bf16[2,512,1024]{2,1,0:T(8,128)(2,1)S(1)} %copy-done), channel_id=1, source_target_pairs={{0,8},{8,0},{16,24},{24,16},{32,40},{40,32},{48,56},{56,48},{64,72... | collective-permute-start | bytes 6291464 | tf_op jit(solution)/shard_map/ppermute | solution.py:480
  117.8 42.0 %collective-permute-start.12 = (bf16[2,128,1024]{2,1,0:T(8,128)(2,1)}, bf16[2,128,1024]{2,1,0:T(8,128)(2,1)S(1)}, u32[]{:S(2)}, u32[]{:S(2)}) collective-permute-start(bf16[2,128,1024]{2,1,0:T(8,128)(2,1)} %constant_dynamic-update-slice_fusion), channel_id=1, source_target_pairs={{0,2},{1,3},{2,0},{3,1},{4,6},{5,7},{6,4},{7,5},{8,10},{9,11},{10,... | collective-permute-start | bytes 1572872 | tf_op jit(solution)/shard_map/ppermute | solution.py:473
  126.4 33.4 %collective-permute-start.11 = (bf16[2,128,1024]{2,1,0:T(8,128)(2,1)}, bf16[2,128,1024]{2,1,0:T(8,128)(2,1)S(1)}, u32[]{:S(2)}, u32[]{:S(2)}) collective-permute-start(bf16[2,128,1024]{2,1,0:T(8,128)(2,1)} %constant_dynamic-update-slice_fusion), channel_id=1, source_target_pairs={{0,3},{1,0},{2,1},{3,2},{4,7},{5,4},{6,5},{7,6},{8,11},{9,8},{10,9... | collective-permute-start | bytes 1572872 | tf_op jit(solution)/shard_map/ppermute | solution.py:473
  131.4 28.4 %collective-permute-start.10 = (bf16[2,128,1024]{2,1,0:T(8,128)(2,1)}, bf16[2,128,1024]{2,1,0:T(8,128)(2,1)}, u32[]{:S(2)}, u32[]{:S(2)}) collective-permute-start(bf16[2,128,1024]{2,1,0:T(8,128)(2,1)} %constant_dynamic-update-slice_fusion), channel_id=1, source_target_pairs={{0,1},{1,2},{2,3},{3,0},{4,5},{5,6},{6,7},{7,4},{8,9},{9,10},{10,1... | collective-permute-start | bytes 1572872 | tf_op jit(solution)/shard_map/ppermute | solution.py:473
  155.2 11.3 %all-to-all-start = ((bf16[8,64,128]{2,1,0:T(8,128)(2,1)}), bf16[8,64,128]{2,1,0:T(8,128)(2,1)S(1)}, u32[]{:S(2)}, u32[]{:S(2)}) async-start(bf16[8,64,128]{2,1,0:T(8,128)(2,1)} %bitcast.19), calls=%async_computation | async-start | bytes 262144 | tf_op jit(solution)/shard_map/all_to_all | solution.py:485
  159.8 6.8 %copy-start.5 = (bf16[2,128,1024]{2,1,0:T(8,128)(2,1)}, bf16[2,128,1024]{2,1,0:T(8,128)(2,1)S(1)}, u32[]{:S(2)}) copy-start(bf16[2,128,1024]{2,1,0:T(8,128)(2,1)S(1)} %collective-permute-done.12.w4) | copy-start | bytes 1572868
  159.8 6.8 %copy-start.6 = (bf16[2,128,1024]{2,1,0:T(8,128)(2,1)}, bf16[2,128,1024]{2,1,0:T(8,128)(2,1)S(1)}, u32[]{:S(2)}) copy-start(bf16[2,128,1024]{2,1,0:T(8,128)(2,1)S(1)} %collective-permute-done.11.w3) | copy-start | bytes 1572868
  166.5 0.7 copy-start.7
  209.3 16.7 %copy-start.10 = (f32[64,1024]{1,0:T(8,128)S(1)}, f32[64,1024]{1,0:T(8,128)}, u32[]{:S(2)}) copy-start(f32[64,1024]{1,0:T(8,128)} %get-tuple-element.69) | copy-start | bytes 786436
